TPU v7x, 32 devices: a whole 2x2x4 slice. The times are simulated.
32 devices in a mesh: seq: 16 (over z, x, core), fsdp: 2 (over y).
Axes of the slice: x: 2, y: 2, z: 4, core: 2. Of those that a mesh axis runs over, the one named last changes fastest.
Arguments:
- tokens: bfloat16 [4096, 1024], P(('seq', 'fsdp')), may hold values from -32 to 32
- doc_bounds: int32 [2, 4096], P(None, ('seq', 'fsdp')), may hold values from 0 to 4096, as said below
- norm_one: bfloat16 [1024], P(('seq', 'fsdp')), may hold values from 0.099609375 to 1.8984375
- w_qkv: bfloat16 [1024, 3072], P(('seq', 'fsdp')), may hold values from -2 to 2
- w_out: bfloat16 [1024, 1024], P(('seq', 'fsdp')), may hold values from -1.5 to 1.5
- norm_two: bfloat16 [1024], P(('seq', 'fsdp')), may hold values from 0.099609375 to 1.8984375
- w_inner: bfloat16 [1024, 5248], P(('seq', 'fsdp')), may hold values from -0.1875 to 0.1875
- w_down: bfloat16 [1024, 2624], P(('seq', 'fsdp')), may hold values from -0.125 to 0.125
- cotangent: bfloat16 [4096, 1024], P(('seq', 'fsdp')), may hold values from -6 to 6
Outputs:
- layer_out: bfloat16 [4096, 1024], P(('seq', 'fsdp'))
- input_grad: float32 [4096, 1024], P(('seq', 'fsdp'))
- norm_one_grad: float32 [1024], P(('seq', 'fsdp'))
- qkv_grad: float32 [1024, 3072], P(('seq', 'fsdp'))
- out_grad: float32 [1024, 1024], P(('seq', 'fsdp'))
- norm_two_grad: float32 [1024], P(('seq', 'fsdp'))
- inner_grad: float32 [1024, 5248], P(('seq', 'fsdp'))
- down_grad: float32 [1024, 2624], P(('seq', 'fsdp'))
Inputs may be any that keep to these rules, and one draw needn't show every extreme that they name: doc_bounds[0, i] and doc_bounds[1, i] are the first index and one past the last index of the document that holds token i; documents are contiguous runs of tokens that together cover all 4096 tokens of the packed stream.
All inputs are finite; a program needn't handle non-finite values.
Results may differ from a plain program's by a relative error of at most 0.014.
Values may be sent and summed in bfloat16 or wider, within the bound.
No kernel may reach another device: no remote copies, remote signals or barrier semaphores. Data moves between devices by JAX's collectives and lax.ppermute only.
A program may use at most 256 MiB of HBM per device.

v0:
```python
import jax
import jax.numpy as jnp
from jax import lax
from jax.sharding import PartitionSpec as P

D = 1024
HEADS = 16
HEAD_DIM = 64
FF = 2624
W = 64


EPS = 1e-05
THETA = 10000.0


def padded_2(value, sides, width):
    for axis, dim in sides:
        size, length = (lax.axis_size(axis), value.shape[dim])
        up = [(i, (i + 1) % size) for i in range(size - 1)]
        down = [(j, i) for i, j in up]
        last = lax.slice_in_dim(value, length - width, length, axis=dim)
        initial = lax.slice_in_dim(value, 0, width, axis=dim)
        before = lax.ppermute(last, axis, up)
        after = lax.ppermute(initial, axis, down)
        value = jnp.concatenate([before, value, after], axis=dim)
    return value


def passed_along(value, axis, by):
    length = lax.axis_size(axis)
    pairs = [(i, i + by) for i in range(length) if 0 <= i + by < length]
    return lax.ppermute(value, axis, pairs)


def normalize(values):
    average = jnp.mean(values, axis=1, keepdims=True)
    centred = values - average
    variance = jnp.mean(centred * centred, axis=1, keepdims=True)
    inverse = lax.rsqrt(variance + EPS)
    return (centred * inverse, inverse)


def normalize_back(grad_rows, normed, inverse, gain):
    scaled = grad_rows * gain
    mean_plain = jnp.mean(scaled, axis=1, keepdims=True)
    mean_cross = jnp.mean(scaled * normed, axis=1, keepdims=True)
    return (
        inverse * (scaled - mean_plain - normed * mean_cross),
        jnp.sum(grad_rows * normed, axis=0),
    )


def rotary_tables(positions):
    half_dim = HEAD_DIM // 2
    freqs = jnp.exp(-jnp.log(THETA) * 2.0 * jnp.arange(half_dim, dtype=jnp.float32) / HEAD_DIM)
    angles = positions[:, None] * freqs[None, :]
    return (jnp.cos(angles)[:, None, :], jnp.sin(angles)[:, None, :])


def rotate(values, cosine, sine):
    half_dim = HEAD_DIM // 2
    front_half = values[..., :half_dim]
    back_half = values[..., half_dim:]
    return jnp.concatenate(
        [front_half * cosine - back_half * sine, back_half * cosine + front_half * sine], axis=-1
    )


def rotate_back(grads, cosine, sine):
    half_dim = HEAD_DIM // 2
    front_half = grads[..., :half_dim]
    back_half = grads[..., half_dim:]
    return jnp.concatenate(
        [front_half * cosine + back_half * sine, back_half * cosine - front_half * sine], axis=-1
    )


def band_scores(queries, keys, visible):
    scores = jnp.einsum(
        "qhd,khd->hqk", queries, keys, preferred_element_type=jnp.float32
    ) * HEAD_DIM ** (-0.5)
    return jnp.where(visible[None], scores, -1e30)


def attend(queries, keys, values, visible):
    scores = band_scores(queries, keys, visible)
    highest = jnp.max(scores, axis=2, keepdims=True)
    summed = jnp.sum(jnp.exp(scores - highest), axis=2, keepdims=True)
    log_total = highest + jnp.log(summed)
    weights = jnp.exp(scores - log_total).astype(jnp.bfloat16)
    mixed = jnp.einsum("hqk,khd->qhd", weights, values, preferred_element_type=jnp.float32)
    return (mixed.astype(jnp.bfloat16), log_total)


def attend_back(queries, keys, values, mixed, grad_mixed, log_total, visible):
    scores = band_scores(queries, keys, visible)
    probs = jnp.exp(scores - log_total)
    weights = probs.astype(jnp.bfloat16)
    grad_probs = jnp.einsum("qhd,khd->hqk", grad_mixed, values, preferred_element_type=jnp.float32)
    delta = jnp.transpose(
        jnp.sum(grad_mixed.astype(jnp.float32) * mixed.astype(jnp.float32), axis=2)
    )[:, :, None]
    grad_scores = (probs * (grad_probs - delta)).astype(jnp.bfloat16)
    grad_queries = jnp.einsum(
        "hqk,khd->qhd", grad_scores, keys, preferred_element_type=jnp.float32
    ) * HEAD_DIM ** (-0.5)
    grad_keys = jnp.einsum(
        "hqk,qhd->khd", grad_scores, queries, preferred_element_type=jnp.float32
    ) * HEAD_DIM ** (-0.5)
    grad_values = jnp.einsum(
        "hqk,qhd->khd", weights, grad_mixed, preferred_element_type=jnp.float32
    )
    return (grad_queries, grad_keys, grad_values)


def contract_rows(left_side, right_side):
    return lax.dot_general(
        left_side, right_side, (((0,), (0,)), ((), ())), preferred_element_type=jnp.float32
    )


def contract_cols(left_side, right_side):
    return lax.dot_general(
        left_side, right_side, (((1,), (1,)), ((), ())), preferred_element_type=jnp.float32
    )


def on_device(tokens, doc_bounds, norm_one, w_qkv, w_out, norm_two, w_inner, w_down, cotangent):
    row_count = tokens.shape[0]
    offset = lax.axis_index(("seq", "fsdp")) * row_count
    gathered = (
        lax.all_gather(norm_one, ("seq", "fsdp"), axis=0, tiled=True),
        lax.all_gather(w_qkv, ("seq", "fsdp"), axis=0, tiled=True),
        lax.all_gather(w_out, ("seq", "fsdp"), axis=0, tiled=True),
        lax.all_gather(norm_two, ("seq", "fsdp"), axis=0, tiled=True),
        lax.all_gather(w_inner, ("seq", "fsdp"), axis=0, tiled=True),
        lax.all_gather(w_down, ("seq", "fsdp"), axis=0, tiled=True),
    )
    gain_low_one, full_qkv, full_out, gain_low_two, full_inner, full_down = gathered
    gain_first = gain_low_one.astype(jnp.float32)
    gain_second = gain_low_two.astype(jnp.float32)
    inputs = tokens.astype(jnp.float32)
    normed_one, inverse_one = normalize(inputs)
    hidden_one = (normed_one * gain_first).astype(jnp.bfloat16)
    projected = jnp.dot(hidden_one, full_qkv, preferred_element_type=jnp.float32)
    token_index = offset + jnp.arange(row_count, dtype=jnp.int32)
    starts = doc_bounds[0]
    ends = doc_bounds[1]
    cosine, sine = rotary_tables((token_index - starts).astype(jnp.float32))
    queries = rotate(projected[:, :D].reshape(row_count, HEADS, HEAD_DIM), cosine, sine).astype(
        jnp.bfloat16
    )
    keys = rotate(projected[:, D : 2 * D].reshape(row_count, HEADS, HEAD_DIM), cosine, sine).astype(
        jnp.bfloat16
    )
    values = projected[:, 2 * D :].astype(jnp.bfloat16)
    local_pair = jnp.concatenate([keys.reshape(row_count, D), values], axis=1)
    padded = padded_2(local_pair, ((("seq", "fsdp"), 0),), W)
    key_count = row_count + 2 * W
    key_index = offset - W + jnp.arange(key_count, dtype=jnp.int32)
    near = jnp.abs(token_index[:, None] - key_index[None, :]) <= W
    inside = (key_index[None, :] >= starts[:, None]) & (key_index[None, :] < ends[:, None])
    visible = near & inside
    all_keys = padded[:, :D].reshape(key_count, HEADS, HEAD_DIM)
    all_values = padded[:, D:].reshape(key_count, HEADS, HEAD_DIM)
    mixed, log_total = attend(queries, all_keys, all_values, visible)
    mixed_flat = mixed.reshape(row_count, D)
    residual = inputs + jnp.dot(mixed_flat, full_out, preferred_element_type=jnp.float32)
    normed_two, inverse_two = normalize(residual)
    hidden_two = (normed_two * gain_second).astype(jnp.bfloat16)
    inner = jnp.dot(hidden_two, full_inner, preferred_element_type=jnp.float32)
    gate_part = inner[:, :FF]
    upward = inner[:, FF:]
    normal_cdf = 0.5 * (1.0 + lax.erf(gate_part * 0.7071067811865476))
    activated = gate_part * normal_cdf
    product = (activated * upward).astype(jnp.bfloat16)
    layer_out = (residual + contract_cols(product, full_down)).astype(jnp.bfloat16)
    back_qkv, back_out, back_inner, back_down = (full_qkv, full_out, full_inner, full_down)
    down_grad = contract_rows(cotangent, product)
    grad_product = jnp.dot(cotangent, back_down, preferred_element_type=jnp.float32)
    gate_slope = normal_cdf + gate_part * jnp.exp(-0.5 * gate_part * gate_part) * 0.3989422804014327
    grad_inner = jnp.concatenate(
        [grad_product * upward * gate_slope, grad_product * activated], axis=1
    ).astype(jnp.bfloat16)
    inner_grad = contract_rows(hidden_two, grad_inner)
    grad_hidden_two = contract_cols(grad_inner, back_inner)
    back_two, norm_two_grad = normalize_back(grad_hidden_two, normed_two, inverse_two, gain_second)
    grad_residual = cotangent.astype(jnp.float32) + back_two
    grad_res_low = grad_residual.astype(jnp.bfloat16)
    out_grad = contract_rows(mixed_flat, grad_res_low)
    grad_mixed = (
        contract_cols(grad_res_low, back_out)
        .astype(jnp.bfloat16)
        .reshape(row_count, HEADS, HEAD_DIM)
    )
    grad_queries, grad_keys, grad_values = attend_back(
        queries, all_keys, all_values, mixed, grad_mixed, log_total, visible
    )
    pair_grads = jnp.concatenate(
        [grad_keys.reshape(key_count, D), grad_values.reshape(key_count, D)], axis=1
    )
    from_upper = passed_along(pair_grads[:W].astype(jnp.bfloat16), ("seq", "fsdp"), -1).astype(
        jnp.float32
    )
    from_lower = passed_along(
        pair_grads[W + row_count :].astype(jnp.bfloat16), ("seq", "fsdp"), 1
    ).astype(jnp.float32)
    own_grads = pair_grads[W : W + row_count]
    own_grads = own_grads.at[row_count - W :].add(from_upper)
    own_grads = own_grads.at[:W].add(from_lower)
    grad_q_raw = rotate_back(grad_queries, cosine, sine).reshape(row_count, D)
    grad_k_raw = rotate_back(
        own_grads[:, :D].reshape(row_count, HEADS, HEAD_DIM), cosine, sine
    ).reshape(row_count, D)
    grad_projected = jnp.concatenate([grad_q_raw, grad_k_raw, own_grads[:, D:]], axis=1).astype(
        jnp.bfloat16
    )
    qkv_grad = contract_rows(hidden_one, grad_projected)
    grad_hidden_one = contract_cols(grad_projected, back_qkv)
    back_one, norm_one_grad = normalize_back(grad_hidden_one, normed_one, inverse_one, gain_first)
    input_grad = grad_residual + back_one
    summed = (
        lax.psum_scatter(norm_one_grad, ("seq", "fsdp"), scatter_dimension=0, tiled=True),
        lax.psum_scatter(qkv_grad, ("seq", "fsdp"), scatter_dimension=0, tiled=True),
        lax.psum_scatter(out_grad, ("seq", "fsdp"), scatter_dimension=0, tiled=True),
        lax.psum_scatter(norm_two_grad, ("seq", "fsdp"), scatter_dimension=0, tiled=True),
        lax.psum_scatter(inner_grad, ("seq", "fsdp"), scatter_dimension=0, tiled=True),
        lax.psum_scatter(down_grad, ("seq", "fsdp"), scatter_dimension=0, tiled=True),
    )
    norm_one_grad, qkv_grad, out_grad, norm_two_grad, inner_grad, down_grad = summed
    return (
        layer_out,
        input_grad,
        norm_one_grad,
        qkv_grad,
        out_grad,
        norm_two_grad,
        inner_grad,
        down_grad,
    )


def solution(mesh):
    placed = (
        P(("seq", "fsdp"), None),
        P(None, ("seq", "fsdp")),
        P(("seq", "fsdp")),
        P(("seq", "fsdp"), None),
        P(("seq", "fsdp"), None),
        P(("seq", "fsdp")),
        P(("seq", "fsdp"), None),
        P(("seq", "fsdp"), None),
        P(("seq", "fsdp"), None),
    )
    return jax.shard_map(
        on_device,
        mesh=mesh,
        in_specs=placed,
        out_specs=(
            P(("seq", "fsdp"), None),
            P(("seq", "fsdp"), None),
            P(("seq", "fsdp")),
            P(("seq", "fsdp"), None),
            P(("seq", "fsdp"), None),
            P(("seq", "fsdp")),
            P(("seq", "fsdp"), None),
            P(("seq", "fsdp"), None),
        ),
        check_vma=False,
    )
```

profile of v0, /device:TPU:0, one launch (start us, length us, event | category | flops | bytes accessed | tf_op | source)
XLA Modules:
  0.0 1240.7 jit_solution(14216436591606232034)
XLA Ops:
  7.9 0.7 all-gather.7.cloned.1.call-update
  10.0 0.8 dynamic-update-slice.6
  10.9 0.8 dynamic-update-slice.7
  11.7 42.5 %all-reduce.5 = (bf16[1024]{0:T(1024)(128)(2,1)S(1)}, bf16[1024]{0:T(1024)(128)(2,1)S(1)}) all-reduce(bf16[1024]{0:T(1024)(128)(2,1)S(1)} %dynamic-update-slice.6, bf16[1024]{0:T(1024)(128)(2,1)S(1)} %dynamic-update-slice.7), channel_id=1, replica_groups=mesh['seq'=16,'fsdp'=2] {'seq','fsdp'}, use_global_device_ids=true, to_apply=%add | all-reduce | flops 2048 | bytes 8192
  54.2 1.1 convert_reduce_fusion
  55.3 1.2 fusion.27
  56.5 0.7 subtract_convert_fusion.4
  57.2 0.8 slice_bitcast_fusion.1
  58.1 24.9 %all-gather.5.cloned.1.call-done = bf16[1024,3072]{1,0:T(8,128)(2,1)} async-done(((bf16[32,3072]{1,0:T(8,128)(2,1)}), bf16[1024,3072]{1,0:T(8,128)(2,1)}) %all-gather.5.cloned.1.call-update) | async-done | bytes 6291472 | tf_op jit(solution)/shard_map/all_gather | solution.py:134
  83.0 3.9 fusion.45
  87.9 1.3 collective-permute-start.1
  89.2 4.7 collective-permute-start
  94.1 4.6 collective-permute-done.1
  98.7 3.4 collective-permute-done
  104.5 38.8 %all-gather.7.cloned.1.call-done = bf16[1024,1024]{1,0:T(8,128)(2,1)} async-done(((bf16[32,1024]{1,0:T(8,128)(2,1)}), bf16[1024,1024]{1,0:T(8,128)(2,1)}) %all-gather.7.cloned.1.call-update) | async-done | bytes 2097168 | tf_op jit(solution)/shard_map/all_gather | solution.py:135
  143.4 2.1 fusion.52
  145.7 86.8 %all-gather.9.cloned.1.call-done = bf16[1024,5248]{1,0:T(8,128)(2,1)} async-done(((bf16[32,5248]{1,0:T(8,128)(2,1)}), bf16[1024,5248]{1,0:T(8,128)(2,1)}) %all-gather.9.cloned.1.call-update) | async-done | bytes 10747920 | tf_op jit(solution)/shard_map/all_gather | solution.py:137
  232.6 7.3 fusion.47
  239.9 60.3 %all-gather.11.cloned.1.call-done = bf16[1024,2624]{1,0:T(8,128)(2,1)} async-done(((bf16[32,2624]{1,0:T(8,128)(2,1)}), bf16[1024,2624]{1,0:T(8,128)(2,1)}) %all-gather.11.cloned.1.call-update) | async-done | bytes 5373968 | tf_op jit(solution)/shard_map/all_gather | solution.py:138
  300.2 4.8 fusion.7
  305.0 8.3 multiply_reduce_fusion
  313.6 2.7 fusion.34
  316.4 7.7 convolution_bitcast_fusion
  324.0 12.0 copy.49
  336.3 3.1 convolution_convert_fusion
  339.5 1.1 copy.46
  340.6 1.0 multiply_reduce_fusion.1
  341.6 1.9 multiply_convert_fusion
  343.9 0.8 fusion.30
  344.8 1.0 fusion.49
  345.9 1.3 collective-permute-start.2
  347.7 5.4 collective-permute-start.3
  353.3 17.3 %collective-permute-done.2 = bf16[64,2048]{0,1:T(8,128)(2,1)S(1)} collective-permute-done((bf16[64,2048]{0,1:T(8,128)(2,1)S(1)}, bf16[64,2048]{0,1:T(8,128)(2,1)S(1)}, u32[]{:S(2)}, u32[]{:S(2)}) %collective-permute-start.2) | collective-permute-done | bytes 262176 | tf_op jit(solution)/shard_map/ppermute | solution.py:33
  370.8 6.1 scatter-add.6
  376.9 2.7 collective-permute-done.3
  379.6 1.1 slice_add_fusion
  380.7 4.5 scatter-add.9
  385.6 6.4 fusion.28
  392.1 1.0 copy-done.22
  393.4 8.9 fusion.13
  402.3 1.7 copy-done
  404.0 5.3 fusion.9
  409.3 5.2 fusion.26
  414.5 55.8 %all-reduce.4 = (f32[1024]{0:T(1024)S(1)}, f32[1024]{0:T(1024)S(1)}) all-reduce(f32[1024]{0:T(1024)S(1)} %get-tuple-element.58, f32[1024]{0:T(1024)S(1)} %get-tuple-element.56), channel_id=2, replica_groups=mesh['seq'=16,'fsdp'=2] {'seq','fsdp'}, use_global_device_ids=true, to_apply=%region_12.13.clone | all-reduce | flops 2048 | bytes 16384
  471.5 1.0 fusion.25
  472.5 143.6 %reduce-scatter.13.cloned.1.call-done = f32[32,2624]{1,0:T(8,128)} async-done(((f32[1024,2624]{1,0:T(8,128)}), f32[32,2624]{1,0:T(8,128)}) %reduce-scatter.13.cloned.1.call-update) | async-done | bytes 335888
  616.1 160.5 %reduce-scatter.7.cloned.1.call-done = f32[32,3072]{1,0:T(8,128)} async-done(((f32[1024,3072]{1,0:T(8,128)}), f32[32,3072]{1,0:T(8,128)}) %reduce-scatter.7.cloned.1.call-update) | async-done | bytes 393232 | tf_op jit(solution)/shard_map/reduce_scatter | solution.py:225
  776.6 457.3 %reduce-scatter.11.cloned.1.call-done = f32[32,5248]{1,0:T(8,128)} async-done(((f32[1024,5248]{1,0:T(8,128)}), f32[32,5248]{1,0:T(8,128)}) %reduce-scatter.11.cloned.1.call-update) | async-done | bytes 671760 | tf_op jit(solution)/shard_map/reduce_scatter | solution.py:228
  (110 shorter events, 9.6 us)
Async XLA Ops:
  7.2 75.8 %all-gather.5.cloned.1.call-start = ((), (), s32[]{:S(2)}) async-start(), calls=%async_computation.4 | async-start | bytes 6488064 | tf_op jit(solution)/shard_map/all_gather | solution.py:134
  7.9 135.5 %all-gather.7.cloned.1.call-start = ((), (), s32[]{:S(2)}) async-start(), calls=%async_computation.5 | async-start | bytes 2162688 | tf_op jit(solution)/shard_map/all_gather | solution.py:135
  8.6 223.9 %all-gather.9.cloned.1.call-start = ((), (), s32[]{:S(2)}) async-start(), calls=%async_computation.6 | async-start | bytes 11083776 | tf_op jit(solution)/shard_map/all_gather | solution.py:137
  9.4 290.8 %all-gather.11.cloned.1.call-start = ((), (), s32[]{:S(2)}) async-start(), calls=%async_computation.7 | async-start | bytes 5677056 | tf_op jit(solution)/shard_map/all_gather | solution.py:138
  10.0 462.6 %reduce-scatter.9.cloned.1.call-start = ((), (), s32[]{:S(2)}) async-start(), calls=%async_computation.9 | async-start | bytes 4325376 | tf_op jit(solution)/shard_map/reduce_scatter | solution.py:226
  87.6 15.0 %copy-start.9 = (bf16[128,16,32]{0,2,1:T(8,128)(2,1)}, bf16[128,16,32]{0,2,1:T(8,128)(2,1)S(1)}, u32[]{:S(2)}) copy-start(bf16[128,16,32]{0,2,1:T(8,128)(2,1)S(1)} %get-tuple-element.78) | copy-start | bytes 393220
  87.6 15.0 %copy-start.11 = (bf16[128,16,32]{0,2,1:T(8,128)(2,1)}, bf16[128,16,32]{0,2,1:T(8,128)(2,1)S(1)}, u32[]{:S(2)}) copy-start(bf16[128,16,32]{0,2,1:T(8,128)(2,1)S(1)} %get-tuple-element.79) | copy-start | bytes 393220
  87.9 10.8 collective-permute-start.1
  89.2 12.9 %collective-permute-start = (bf16[64,2048]{1,0:T(8,128)(2,1)S(1)}, bf16[64,2048]{1,0:T(8,128)(2,1)S(1)}, u32[]{:S(2)}, u32[]{:S(2)}) collective-permute-start(bf16[64,2048]{1,0:T(8,128)(2,1)S(1)} %get-tuple-element.82), channel_id=1, source_target_pairs={{0,1},{1,2},{2,3},{3,4},{4,5},{5,6},{6,7},{7,8},{8,9},{9,10},{10,1... | collective-permute-start | bytes 786440 | tf_op jit(solution)/shard_map/ppermute | solution.py:24
  102.4 1.5 copy-start.4
  102.6 1.3 copy-start.5
  103.2 40.1 %copy-start.1 = (bf16[128,1024]{1,0:T(8,128)(2,1)S(1)}, bf16[128,1024]{1,0:T(8,128)(2,1)}, u32[]{:S(2)}) copy-start(bf16[128,1024]{1,0:T(8,128)(2,1)} %param.13) | copy-start | bytes 786436
  104.5 135.4 %copy-start.7 = (bf16[16,64,128]{2,1,0:T(8,128)(2,1)}, bf16[16,64,128]{2,1,0:T(8,128)(2,1)S(1)}, u32[]{:S(2)}) copy-start(bf16[16,64,128]{2,1,0:T(8,128)(2,1)S(1)} %convolution_convert_fusion.1) | copy-start | bytes 786436
  145.7 154.5 %copy-start.13 = (bf16[128,1024]{1,0:T(8,128)(2,1)S(1)}, bf16[128,1024]{1,0:T(8,128)(2,1)}, u32[]{:S(2)}) copy-start(bf16[128,1024]{1,0:T(8,128)(2,1)} %param.21) | copy-start | bytes 786436
  305.0 8.3 copy-start.21
  305.0 8.3 copy-start.23
  305.0 8.3 copy-start.14
  305.0 8.6 copy-start.8
  313.6 22.7 %copy-start.2 = (f32[128,1024]{1,0:T(8,128)}, f32[128,1024]{1,0:T(8,128)S(1)}, u32[]{:S(2)}) copy-start(f32[128,1024]{1,0:T(8,128)S(1)} %multiply_add_fusion) | copy-start | bytes 1572868
  316.3 299.8 %reduce-scatter.13.cloned.1.call-start = ((), (), s32[]{:S(2)}) async-start(), calls=%async_computation.11 | async-start | bytes 11354112
  336.0 440.5 %reduce-scatter.7.cloned.1.call-start = ((), (), s32[]{:S(2)}) async-start(), calls=%async_computation.8 | async-start | bytes 12976128 | tf_op jit(solution)/shard_map/reduce_scatter | solution.py:225
  341.6 1.9 copy-start.10
  341.6 1.9 copy-start.12
  344.7 2.5 copy-start.6
  345.9 24.8 %collective-permute-start.2 = (bf16[64,2048]{0,1:T(8,128)(2,1)S(1)}, bf16[64,2048]{0,1:T(8,128)(2,1)S(1)}, u32[]{:S(2)}, u32[]{:S(2)}) collective-permute-start(bf16[64,2048]{0,1:T(8,128)(2,1)S(1)} %get-tuple-element.71), channel_id=1, source_target_pairs={{1,0},{2,1},{3,2},{4,3},{5,4},{6,5},{7,6},{8,7},{9,8},{10,9},{11,1... | collective-permute-start | bytes 786440 | tf_op jit(solution)/shard_map/ppermute | solution.py:33
  347.7 31.9 %collective-permute-start.3 = (bf16[64,2048]{0,1:T(8,128)(2,1)}, bf16[64,2048]{0,1:T(8,128)(2,1)}, u32[]{:S(2)}, u32[]{:S(2)}) collective-permute-start(bf16[64,2048]{0,1:T(8,128)(2,1)} %get-tuple-element.70), channel_id=1, source_target_pairs={{0,1},{1,2},{2,3},{3,4},{4,5},{5,6},{6,7},{7,8},{8,9},{9,10},{10,1... | collective-permute-start | bytes 786440 | tf_op jit(solution)/shard_map/ppermute | solution.py:33
  385.3 6.7 copy-start.15
  385.5 6.5 copy-start.17
  385.6 6.5 copy-start.19
  392.0 1.1 copy-start.22
  392.0 1.3 copy-start.24
  392.1 841.8 %reduce-scatter.11.cloned.1.call-start = ((), (), s32[]{:S(2)}) async-start(), calls=%async_computation.10 | async-start | bytes 22167552 | tf_op jit(solution)/shard_map/reduce_scatter | solution.py:228
  402.3 1.8 copy-start
  404.0 5.3 copy-start.16
  404.0 5.3 copy-start.18
  404.0 5.3 copy-start.20
  409.3 62.1 %copy-start.3 = (f32[128,1024]{1,0:T(8,128)S(1)}, f32[128,1024]{1,0:T(8,128)}, u32[]{:S(2)}) copy-start(f32[128,1024]{1,0:T(8,128)} %copy-done.2) | copy-start | bytes 1572868
Sparse Core Ops, SparseCore 0:
  10.9 72.0 all-gather.4
  86.1 57.2 all-gather.6
  146.2 86.3 all-gather.8
  235.4 64.7 all-gather.10
  316.5 150.5 reduce-scatter.8
  473.4 142.6 reduce-scatter.12
  622.7 153.8 reduce-scatter.6
  779.5 454.3 reduce-scatter.10
where the time goes:
time: 1240 us
  waiting for transfers between devices  1000 us (81%)
  blocking collectives  98.3 us (8%)
  matrix products  70.4 us (6%)
  local copies, waits for them, and re-layouts  32.6 us (3%)
  between operations  14.7 us (1%)
  starting transfers between devices  13.2 us (1%)
    reduce_scatter x1, waiting for transfers between devices, on_device(): lax.psum_scatter(inner_grad, ('seq', 'fsdp'), scatter_dimension=0, tiled=...  457 us
    reduce_scatter x1, waiting for transfers between devices, on_device(): lax.psum_scatter(qkv_grad, ('seq', 'fsdp'), scatter_dimension=0, tiled=True)  160 us
    unnamed x9, waiting for transfers between devices  146 us
    unnamed x2, blocking collectives  98.3 us
    all_gather x1, waiting for transfers between devices, on_device(): lax.all_gather(w_inner, ('seq', 'fsdp'), axis=0, tiled=True)  86.8 us
    all_gather x1, waiting for transfers between devices, on_device(): lax.all_gather(w_down, ('seq', 'fsdp'), axis=0, tiled=True)  60.3 us
    all_gather x1, waiting for transfers between devices, on_device(): lax.all_gather(w_out, ('seq', 'fsdp'), axis=0, tiled=True)  38.8 us
    dot_general x4, matrix products, contract_rows(): lax.dot_general(left_side, right_side, (((0,), (0,)), ((), ())), preferre...  25.7 us
  transfers between devices with their start and end apart: 12, of which 11 were waited for; matrix products, arithmetic and copies ran while one was open for 7% of the time, Pallas kernels for 0%

commit v1 on v0

v1 whole, which is shorter than its diff:
```python
import functools

import jax
import jax.numpy as jnp
from jax import lax
from jax.experimental import pallas as pl
from jax.experimental.pallas import tpu as pltpu
from jax.sharding import Mesh, PartitionSpec as P

HEAD_DIM = 64
W = 64
EPS = 1e-05
THETA = 10000.0
TP = 8
LANES = 128
ORDER = (0, 1, 4, 5, 2, 3, 6, 7)

bf16 = jnp.bfloat16
f32 = jnp.float32
PLANE = ("a", "c", "b")
ALL = ("g", "a", "c", "b")


def swap(value, axis):
    return lax.ppermute(value, axis, [(0, 1), (1, 0)])


def swap_both(value):
    return lax.ppermute(value, ("a", "b"), [(i, 3 - i) for i in range(4)])


def gather_plane(own):
    quad = [own, swap(own, "b"), swap(own, "a"), swap_both(own)]
    return jnp.concatenate(quad + [swap(q, "c") for q in quad], axis=0)


def scatter_plane(parts, rows):
    piece = [parts[i * rows : (i + 1) * rows] for i in range(TP)]
    pair = [piece[q].astype(f32) + swap(piece[4 + q], "c").astype(f32) for q in range(4)]
    return (
        pair[0]
        + swap(pair[1].astype(bf16), "b").astype(f32)
        + swap(pair[2].astype(bf16), "a").astype(f32)
        + swap_both(pair[3].astype(bf16)).astype(f32)
    )


def position_of(block, me):
    x = block ^ me
    return ((x >> 1) & 1) * 4 + ((x >> 2) & 1) * 2 + (x & 1)


def swap_halves(u):
    lane = lax.broadcasted_iota(jnp.int32, u.shape, 1)
    return jnp.where((lane & 63) < 32, pltpu.roll(u, 96, 1), pltpu.roll(u, 32, 1))


def project_body(x_ref, w_ref, cos_ref, sin_ref, n_ref, q_ref, k_ref, v_ref):
    x = x_ref[...].astype(f32)
    mean = jnp.mean(x, axis=1, keepdims=True)
    centred = x - mean
    var = jnp.mean(centred * centred, axis=1, keepdims=True)
    normed = (centred * lax.rsqrt(var + EPS)).astype(bf16)
    n_ref[...] = normed
    out = jnp.dot(normed, w_ref[...], preferred_element_type=f32)
    c = cos_ref[...]
    s = sin_ref[...]
    q = out[:, :LANES]
    k = out[:, LANES : 2 * LANES]
    q_ref[...] = (q * c + swap_halves(q) * s).astype(bf16)
    k_ref[...] = (k * c + swap_halves(k) * s).astype(bf16)
    v_ref[...] = out[:, 2 * LANES :].astype(bf16)


def project(x, w, cosine, sine, rows):
    total, dim = x.shape
    row = lambda i: (i, 0)
    lane_spec = pl.BlockSpec((rows, LANES), row)
    return pl.pallas_call(
        project_body,
        grid=(total // rows,),
        in_specs=[
            pl.BlockSpec((rows, dim), row),
            pl.BlockSpec((dim, 3 * LANES), lambda i: (0, 0)),
            lane_spec,
            lane_spec,
        ],
        out_specs=[pl.BlockSpec((rows, dim), row), lane_spec, lane_spec, lane_spec],
        out_shape=[jax.ShapeDtypeStruct((total, dim), bf16)]
        + [jax.ShapeDtypeStruct((total, LANES), bf16)] * 3,
        name="project",
    )(x, w, cosine, sine)


def fill_window(dst, src, before, after, me, rows):
    dst[0:W, :] = before
    for j in range(TP):
        at = pl.multiple_of(position_of(j, me) * rows, rows)
        dst[W + j * rows : W + (j + 1) * rows, :] = src[pl.ds(at, rows), :]
    dst[W + TP * rows : 2 * W + TP * rows, :] = after


def visible_of(st, en, first, rows):
    shape = (rows, rows + 2 * W)
    query = lax.broadcasted_iota(jnp.int32, shape, 0)
    key = lax.broadcasted_iota(jnp.int32, shape, 1)
    gap = key - query
    at = key + (first - W)
    return (gap >= 0) & (gap <= 2 * W) & (at >= st) & (at < en)


def keep_head(value, head):
    lane = lax.broadcasted_iota(jnp.int32, value.shape, 1)
    return jnp.where((lane >= HEAD_DIM) == (head == 1), value, jnp.zeros_like(value))


def pick_head(zero, one):
    lane = lax.broadcasted_iota(jnp.int32, (zero.shape[0], LANES), 1)
    return jnp.where(lane < HEAD_DIM, zero, one)


def dot_t(x, y):
    return lax.dot_general(x, y, (((1,), (1,)), ((), ())), preferred_element_type=f32)


def dot_rows(x, y):
    return lax.dot_general(x, y, (((0,), (0,)), ((), ())), preferred_element_type=f32)


def attend_body(rows, at_ref, q_ref, k_ref, v_ref, hb_ref, ha_ref, st_ref, en_ref, o_ref, l_ref, kw, vw):
    me = at_ref[0]
    base = at_ref[1]
    fill_window(kw, k_ref, hb_ref[:, :LANES], ha_ref[:, :LANES], me, rows)
    fill_window(vw, v_ref, hb_ref[:, LANES:], ha_ref[:, LANES:], me, rows)
    for j in range(TP):
        at = pl.multiple_of(position_of(j, me) * rows, rows)
        q = q_ref[pl.ds(at, rows), :]
        k = kw[j * rows : (j + 1) * rows + 2 * W, :]
        v = vw[j * rows : (j + 1) * rows + 2 * W, :]
        vis = visible_of(st_ref[pl.ds(at, rows), :], en_ref[pl.ds(at, rows), :], base + j * rows, rows)
        outs = []
        logs = []
        for h in range(2):
            s = jnp.where(vis, dot_t(keep_head(q, h), k) * HEAD_DIM ** (-0.5), -1e30)
            top = jnp.max(s, axis=1, keepdims=True)
            log_total = top + jnp.log(jnp.sum(jnp.exp(s - top), axis=1, keepdims=True))
            p = jnp.exp(s - log_total).astype(bf16)
            outs.append(jnp.dot(p, v, preferred_element_type=f32))
            logs.append(log_total)
        o_ref[pl.ds(at, rows), :] = pick_head(*outs).astype(bf16)
        l_ref[pl.ds(at, rows), :] = pick_head(*logs)


def attend(place, q, k, v, before, after, st, en, rows):
    total = q.shape[0]
    vm = pl.BlockSpec(memory_space=pltpu.VMEM)
    return pl.pallas_call(
        functools.partial(attend_body, rows),
        in_specs=[pl.BlockSpec(memory_space=pltpu.SMEM)] + [vm] * 7,
        out_specs=[vm, vm],
        out_shape=[jax.ShapeDtypeStruct((total, LANES), bf16), jax.ShapeDtypeStruct((total, LANES), f32)],
        scratch_shapes=[pltpu.VMEM((total + 2 * W, LANES), bf16)] * 2,
        name="attend",
    )(place, q, k, v, before, after, st, en)


def attend_back_body(
    rows, at_ref, q_ref, k_ref, v_ref, hb_ref, ha_ref, st_ref, en_ref, o_ref, l_ref, g_ref, cos_ref, sin_ref,
    dq_ref, dk_ref, dv_ref, kw, vw,
):
    me = at_ref[0]
    base = at_ref[1]
    fill_window(kw, k_ref, hb_ref[:, :LANES], ha_ref[:, :LANES], me, rows)
    fill_window(vw, v_ref, hb_ref[:, LANES:], ha_ref[:, LANES:], me, rows)
    dk_ref[...] = jnp.zeros_like(dk_ref)
    dv_ref[...] = jnp.zeros_like(dv_ref)
    scale = HEAD_DIM ** (-0.5)
    for j in range(TP):
        at = pl.multiple_of(position_of(j, me) * rows, rows)
        sl = slice(j * rows, (j + 1) * rows + 2 * W)
        q = q_ref[pl.ds(at, rows), :]
        k = kw[sl, :]
        v = vw[sl, :]
        g = g_ref[pl.ds(at, rows), :]
        both = g.astype(f32) * o_ref[pl.ds(at, rows), :].astype(f32)
        logs = l_ref[pl.ds(at, rows), :]
        vis = visible_of(st_ref[pl.ds(at, rows), :], en_ref[pl.ds(at, rows), :], base + j * rows, rows)
        dqs = []
        dk = jnp.zeros((rows + 2 * W, LANES), f32)
        dv = jnp.zeros((rows + 2 * W, LANES), f32)
        for h in range(2):
            qh = keep_head(q, h)
            gh = keep_head(g, h)
            s = jnp.where(vis, dot_t(qh, k) * scale, -1e30)
            p = jnp.exp(s - logs[:, h * HEAD_DIM : h * HEAD_DIM + 1])
            delta = jnp.sum(keep_head(both, h), axis=1, keepdims=True)
            ds = (p * (dot_t(gh, v) - delta)).astype(bf16)
            dqs.append(jnp.dot(ds, k, preferred_element_type=f32))
            dk = dk + dot_rows(ds, qh)
            dv = dv + dot_rows(p.astype(bf16), gh)
        dq = pick_head(*dqs) * scale
        c = cos_ref[pl.ds(at, rows), :]
        s = sin_ref[pl.ds(at, rows), :]
        dq_ref[pl.ds(at, rows), :] = (dq * c - swap_halves(dq) * s).astype(bf16)
        dk_ref[sl, :] += dk * scale
        dv_ref[sl, :] += dv


def attend_back(place, q, k, v, before, after, st, en, o, logs, g, cosine, sine, rows):
    total = q.shape[0]
    vm = pl.BlockSpec(memory_space=pltpu.VMEM)
    wide = jax.ShapeDtypeStruct((total + 2 * W, LANES), f32)
    return pl.pallas_call(
        functools.partial(attend_back_body, rows),
        in_specs=[pl.BlockSpec(memory_space=pltpu.SMEM)] + [vm] * 12,
        out_specs=[vm] * 3,
        out_shape=[jax.ShapeDtypeStruct((total, LANES), bf16), wide, wide],
        scratch_shapes=[pltpu.VMEM((total + 2 * W, LANES), bf16)] * 2,
        name="attend_back",
    )(place, q, k, v, before, after, st, en, o, logs, g, cosine, sine)


def finish_body(rows, at_ref, dq_ref, dk_ref, dv_ref, fb_ref, fa_ref, cos_ref, sin_ref, out_ref):
    me = at_ref[0]
    for j in range(TP):
        at = pl.multiple_of(position_of(j, me) * rows, rows)
        dk = dk_ref[W + j * rows : W + (j + 1) * rows, :]
        dv = dv_ref[W + j * rows : W + (j + 1) * rows, :]
        rest = jnp.zeros((rows - W, LANES), f32)
        if j == 0:
            both = fb_ref[...].astype(f32)
            dk = dk + jnp.concatenate([both[:, :LANES], rest], axis=0)
            dv = dv + jnp.concatenate([both[:, LANES:], rest], axis=0)
        if j == TP - 1:
            both = fa_ref[...].astype(f32)
            dk = dk + jnp.concatenate([rest, both[:, :LANES]], axis=0)
            dv = dv + jnp.concatenate([rest, both[:, LANES:]], axis=0)
        c = cos_ref[pl.ds(at, rows), :]
        s = sin_ref[pl.ds(at, rows), :]
        out_ref[pl.ds(at, rows), 0:LANES] = dq_ref[pl.ds(at, rows), :]
        out_ref[pl.ds(at, rows), LANES : 2 * LANES] = (dk * c - swap_halves(dk) * s).astype(bf16)
        out_ref[pl.ds(at, rows), 2 * LANES : 3 * LANES] = dv.astype(bf16)


def finish(place, dq, dk, dv, from_before, from_after, cosine, sine, rows):
    vm = pl.BlockSpec(memory_space=pltpu.VMEM)
    return pl.pallas_call(
        functools.partial(finish_body, rows),
        in_specs=[pl.BlockSpec(memory_space=pltpu.SMEM)] + [vm] * 7,
        out_specs=vm,
        out_shape=jax.ShapeDtypeStruct((dq.shape[0], 3 * LANES), bf16),
        name="finish",
    )(place, dq, dk, dv, from_before, from_after, cosine, sine)


def along(value, groups, by):
    return lax.ppermute(value, "g", [(i, i + by) for i in range(groups) if 0 <= i + by < groups])


def spread_groups(mine, groups):
    copies = jnp.broadcast_to(mine[None], (groups,) + mine.shape)
    got = lax.all_to_all(copies, "g", 0, 0, tiled=True)
    return got.reshape((groups * mine.shape[0],) + mine.shape[1:])


def columns_to_plane(blocks):
    got = lax.all_to_all(blocks, PLANE, 0, 0, tiled=True)
    return got.reshape((blocks.shape[0] * blocks.shape[1], blocks.shape[2]))


def layer_norm(values):
    average = jnp.mean(values, axis=1, keepdims=True)
    centred = values - average
    variance = jnp.mean(centred * centred, axis=1, keepdims=True)
    inverse = lax.rsqrt(variance + EPS)
    return (centred * inverse, inverse)


def layer_norm_back(scaled, normed, inverse):
    mean_plain = jnp.mean(scaled, axis=1, keepdims=True)
    mean_cross = jnp.mean(scaled * normed, axis=1, keepdims=True)
    return inverse * (scaled - mean_plain - normed * mean_cross)


def low_dot(x, y):
    return jnp.dot(x, y, preferred_element_type=f32)


def to_owners(grad, count, groups):
    own_rows, cols = grad.shape[0] // count, grad.shape[1]
    got = lax.all_to_all(grad.astype(bf16).reshape(count, own_rows, cols), ALL, 0, 0, tiled=True)
    return jnp.sum(got.reshape(groups, TP, own_rows, cols).astype(f32), axis=0)


def on_device(tokens, doc_bounds, norm_one, w_qkv, w_out, norm_two, w_inner, w_down, cotangent):
    rows, dim = tokens.shape
    own_rows = w_qkv.shape[0]
    ff = w_down.shape[1]
    groups = lax.axis_size("g")
    count = groups * TP
    group = lax.axis_index("g")
    me = lax.axis_index(PLANE)
    part = ff // TP
    wide = -(-part // LANES) * LANES
    base = group * (TP * rows)
    place = jnp.stack([me, base]).astype(jnp.int32)

    gain_one = norm_one.astype(f32)[:, None]
    gain_two = norm_two.astype(f32)[:, None]

    x_all = gather_plane(tokens)
    bounds = gather_plane(doc_bounds[None])
    qkv_mine = (w_qkv.astype(f32) * gain_one).astype(bf16).reshape(own_rows, 3, TP, LANES)
    qkv_mine = jnp.transpose(qkv_mine, (2, 0, 1, 3)).reshape(TP, own_rows, 3 * LANES)
    wq = spread_groups(columns_to_plane(qkv_mine), groups)

    def padded(mat):
        cut = jnp.transpose(mat.reshape(own_rows, TP, part), (1, 0, 2))
        return jnp.pad(cut, ((0, 0), (0, 0), (0, wide - part)))

    scaled_inner = (w_inner.astype(f32) * gain_two).astype(bf16)
    ff_mine = jnp.concatenate(
        [padded(scaled_inner[:, :ff]), padded(scaled_inner[:, ff:]), padded(w_down)], axis=2
    )
    wf = spread_groups(columns_to_plane(ff_mine), groups)
    w_both = wf[:, : 2 * wide]
    w_dn = wf[:, 2 * wide :]

    wo = jnp.zeros((own_rows * groups, dim), bf16)
    for k in range(groups):
        pairs = [(s, ((s % groups - k) % groups) * TP + s // groups) for s in range(count)]
        got = lax.ppermute(w_out, ALL, pairs)
        wo = lax.dynamic_update_slice(wo, got, (((group + k) % groups) * own_rows, 0))

    c_all = gather_plane(cotangent)

    start = bounds[:, 0, :].reshape(TP * rows, 1)
    end = bounds[:, 1, :].reshape(TP * rows, 1)
    slot = jnp.array(ORDER, jnp.int32)
    index = (base + (slot ^ me)[:, None] * rows + jnp.arange(rows, dtype=jnp.int32)[None, :]).reshape(TP * rows, 1)
    lane = jnp.arange(LANES, dtype=jnp.int32)
    half = HEAD_DIM // 2
    freqs = jnp.exp(-jnp.log(THETA) * 2.0 * (lane % half).astype(f32) / HEAD_DIM)
    angles = (index - start).astype(f32) * freqs[None, :]
    cosine = jnp.cos(angles)
    sine = jnp.sin(angles) * jnp.where(lane % HEAD_DIM < half, -1.0, 1.0)[None, :]

    n1, q, k, v = project(x_all, wq, cosine, sine, rows)
    at_first = position_of(0, me) * rows
    at_last = position_of(TP - 1, me) * rows + rows - W
    kv_first = jnp.concatenate([lax.dynamic_slice(t, (at_first, 0), (W, LANES)) for t in (k, v)], axis=1)
    kv_last = jnp.concatenate([lax.dynamic_slice(t, (at_last, 0), (W, LANES)) for t in (k, v)], axis=1)
    before = along(kv_last, groups, 1)
    after = along(kv_first, groups, -1)
    mixed, logs = attend(place, q, k, v, before, after, start, end, rows)
    inputs = tokens.astype(f32)
    residual = inputs + scatter_plane(low_dot(mixed, wo).astype(bf16), rows)
    normed_two, inverse_two = layer_norm(residual)
    n2 = gather_plane(normed_two.astype(bf16))

    inner = low_dot(n2, w_both)
    gate = inner[:, :wide]
    upward = inner[:, wide:]
    cdf = 0.5 * (1.0 + lax.erf(gate * 0.7071067811865476))
    activated = gate * cdf
    product = (activated * upward).astype(bf16)
    grad_product = low_dot(c_all, w_dn)
    slope = cdf + gate * jnp.exp(-0.5 * gate * gate) * 0.3989422804014327
    grad_inner = jnp.concatenate(
        [grad_product * upward * slope, grad_product * activated], axis=1
    ).astype(bf16)
    grad_scaled_two = scatter_plane(dot_t(grad_inner, w_both).astype(bf16), rows)
    layer_out = (residual + scatter_plane(dot_t(product, w_dn).astype(bf16), rows)).astype(bf16)
    ff_grad = to_owners(
        jnp.concatenate([dot_rows(n2, grad_inner).astype(bf16), dot_rows(c_all, product).astype(bf16)], axis=1),
        count,
        groups,
    )
    grad_residual = cotangent.astype(f32) + layer_norm_back(grad_scaled_two, normed_two, inverse_two)
    r_all = gather_plane(grad_residual.astype(bf16))

    grad_mixed = dot_t(r_all, wo).astype(bf16)
    dq, dk, dv = attend_back(place, q, k, v, before, after, start, end, mixed, logs, grad_mixed, cosine, sine, rows)
    pair = jnp.concatenate([dk, dv], axis=1)
    from_after = along(pair[:W].astype(bf16), groups, -1)
    from_before = along(pair[W + TP * rows :].astype(bf16), groups, 1)
    grad_projected = finish(place, dq, dk, dv, from_before, from_after, cosine, sine, rows)

    out_part = dot_rows(mixed, r_all).astype(bf16)
    out_grad = jnp.zeros((own_rows, dim), f32)
    for k_at in range(groups):
        pairs = [(z * TP + p, groups * p + (z + k_at) % groups) for z in range(groups) for p in range(TP)]
        cut = lax.dynamic_slice(out_part, (((group + k_at) % groups) * own_rows, 0), (own_rows, dim))
        out_grad = out_grad + lax.ppermute(cut, ALL, pairs).astype(f32)

    grad_scaled_one = scatter_plane(dot_t(grad_projected, wq).astype(bf16), rows)
    normed_one, inverse_one = layer_norm(inputs)
    input_grad = grad_residual + layer_norm_back(grad_scaled_one, normed_one, inverse_one)

    qkv_raw = to_owners(dot_rows(n1, grad_projected), count, groups)
    qkv_raw = jnp.transpose(qkv_raw.reshape(TP, own_rows, 3, LANES), (1, 2, 0, 3)).reshape(own_rows, 3 * dim)
    norm_one_grad = jnp.sum(qkv_raw * w_qkv.astype(f32), axis=1)
    qkv_grad = qkv_raw * gain_one

    def joined(at):
        cut = ff_grad[:, :, at * wide : at * wide + part]
        return jnp.transpose(cut, (1, 0, 2)).reshape(own_rows, ff)

    inner_raw = jnp.concatenate([joined(0), joined(1)], axis=1)
    norm_two_grad = jnp.sum(inner_raw * w_inner.astype(f32), axis=1)
    inner_grad = inner_raw * gain_two
    return (layer_out, input_grad, norm_one_grad, qkv_grad, out_grad, norm_two_grad, inner_grad, joined(2))


def solution(mesh):
    devices = mesh.devices.reshape(-1, 2, 2, 2)
    fine = Mesh(devices, ALL)
    row = P(ALL, None)
    vec = P(ALL)
    return jax.shard_map(
        on_device,
        mesh=fine,
        in_specs=(row, P(None, ALL), vec, row, row, vec, row, row, row),
        out_specs=(row, row, vec, row, row, vec, row, row),
        check_vma=False,
    )
```

time: 1240 us -> 356 us (0.29)
  waiting for transfers between devices: 1000 us -> 93.8 us
  starting transfers between devices: 13.2 us -> 146 us
  blocking collectives: 98.3 us -> 0 us
  matrix products: 70.4 us -> 27.9 us
  Pallas kernels: 0 us -> 22.6 us
  other arithmetic: 8.62 us -> 22.1 us
  between operations: 14.7 us -> 2.28 us
    reduce_scatter x3 -> x0, waiting for transfers between devices: 618 us -> none  [the longest x1 457 us: on_device(): lax.psum_scatter(inner_grad, ('seq', 'fsdp'), scatter_dimension=0, tiled=...]
    all_gather x4 -> x0, waiting for transfers between devices: 211 us -> none  [the longest x1 86.8 us: on_device(): lax.all_gather(w_inner, ('seq', 'fsdp'), axis=0, tiled=True)]
    unnamed x9 -> x0, waiting for transfers between devices: 146 us -> none
    ppermute x4 -> x75, starting transfers between devices: 12.7 us -> 119 us  [the longest x9 52 us: swap_both(): return lax.ppermute(value, ('a', 'b'), [(i, 3 - i) for i in range(4)])]
    unnamed x2 -> x0, blocking collectives: 98.3 us -> none
    ppermute x4 -> x75, waiting for transfers between devices: 28 us -> 72.3 us  [the longest x54 52.9 us: swap(): return lax.ppermute(value, axis, [(0, 1), (1, 0)])]
    dot_general x18 -> x11, matrix products: 70.4 us -> 27.9 us  [the longest x4 9.57 us: dot_rows(): lax.dot_general(x, y, (((0,), (0,)), ((), ())), preferred_element_type=f32)]
    all_to_all x0 -> x6, starting transfers between devices: none -> 26.4 us  [the longest x2 9.95 us: spread_groups(): got = lax.all_to_all(copies, 'g', 0, 0, tiled=True)]
  transfers between devices with their start and end apart: 12 -> 81, of which waited for: 11 -> 27; matrix products, arithmetic and copies ran while one was open for 7% -> 16% of each run, Pallas kernels for 0% -> 4%
where the time goes in v1:
time: 356 us; the launch traced here: 349 us
  starting transfers between devices  146 us (41%)
  waiting for transfers between devices  93.8 us (26%)
  local copies, waits for them, and re-layouts  34.7 us (10%)
  matrix products  27.9 us (8%)
  Pallas kernels  22.6 us (6%)
  other arithmetic  22.1 us (6%)
    ppermute x54, waiting for transfers between devices, swap(): return lax.ppermute(value, axis, [(0, 1), (1, 0)])  52.9 us
    ppermute x9, starting transfers between devices, swap_both(): return lax.ppermute(value, ('a', 'b'), [(i, 3 - i) for i in range(4)])  52 us
    ppermute x54, starting transfers between devices, swap(): return lax.ppermute(value, axis, [(0, 1), (1, 0)])  29.9 us
    ppermute x9, waiting for transfers between devices, swap_both(): return lax.ppermute(value, ('a', 'b'), [(i, 3 - i) for i in range(4)])  15.9 us
    ppermute x4, starting transfers between devices, on_device(): got = lax.ppermute(w_out, ALL, pairs)  15.2 us
    ppermute x4, starting transfers between devices, on_device(): out_grad = out_grad + lax.ppermute(cut, ALL, pairs).astype(f32)  13.8 us
    all_to_all x2, waiting for transfers between devices, spread_groups(): got = lax.all_to_all(copies, 'g', 0, 0, tiled=True)  11.8 us
    unnamed x99, local copies, waits for them, and re-layouts  11.6 us
  transfers between devices with their start and end apart: 81, of which 27 were waited for; matrix products, arithmetic and copies ran while one was open for 16% of the time, Pallas kernels for 4%

profile of v1, /device:TPU:0, one launch (start us, length us, event | category | flops | bytes accessed | tf_op | source)
XLA Modules:
  0.0 349.2 jit_solution(18035453492345617161)
XLA Ops:
  1.2 3.5 %collective-permute-start.9 = (s32[1,2,128]{2,0,1:T(1,128)}, s32[1,2,128]{2,0,1:T(1,128)S(1)}, u32[]{:S(2)}, u32[]{:S(2)}) collective-permute-start(s32[1,2,128]{2,0,1:T(1,128)} %bitcast.73), channel_id=1, source_target_pairs={{0,5},{1,4},{4,1},{5,0},{2,7},{3,6},{6,3},{7,2},{8,13},{9,12},{12,... | collective-permute-start | bytes 3080 | tf_op jit(solution)/shard_map/ppermute | solution.py:29
  5.4 5.9 %collective-permute-start.17 = (bf16[32,1024]{1,0:T(8,128)(2,1)}, bf16[32,1024]{1,0:T(8,128)(2,1)S(1)}, u32[]{:S(2)}, u32[]{:S(2)}) collective-permute-start(bf16[32,1024]{1,0:T(8,128)(2,1)} %param.14), channel_id=1, source_target_pairs={{0,24},{1,0},{2,8},{3,16},{4,25},{5,1},{6,9},{7,17},{8,26},{9,2},{... | collective-permute-start | bytes 196616 | tf_op jit(solution)/shard_map/ppermute | solution.py:332
  14.0 4.2 %all-to-all-start = ((bf16[8,32,384]{2,1,0:T(8,128)(2,1)}), bf16[8,32,384]{2,1,0:T(8,128)(2,1)}, u32[]{:S(2)}, u32[]{:S(2)}) async-start(bf16[8,32,384]{2,1,0:T(8,128)(2,1)} %reshape.158), calls=%async_computation | async-start | bytes 393216 | tf_op jit(solution)/shard_map/all_to_all | solution.py:267
  29.0 4.2 %collective-permute-start.19 = (bf16[32,1024]{1,0:T(8,128)(2,1)}, bf16[32,1024]{1,0:T(8,128)(2,1)S(1)}, u32[]{:S(2)}, u32[]{:S(2)}) collective-permute-start(bf16[32,1024]{1,0:T(8,128)(2,1)} %param.14), channel_id=1, source_target_pairs={{0,8},{1,16},{2,24},{3,0},{4,9},{5,17},{6,25},{7,1},{8,10},{9,18},... | collective-permute-start | bytes 196616 | tf_op jit(solution)/shard_map/ppermute | solution.py:332
  33.1 3.7 %collective-permute-start.18 = (bf16[32,1024]{1,0:T(8,128)(2,1)}, bf16[32,1024]{1,0:T(8,128)(2,1)}, u32[]{:S(2)}, u32[]{:S(2)}) collective-permute-start(bf16[32,1024]{1,0:T(8,128)(2,1)} %param.14), channel_id=1, source_target_pairs={{0,16},{1,24},{2,0},{3,8},{4,17},{5,25},{6,1},{7,9},{8,18},{9,26},... | collective-permute-start | bytes 196616 | tf_op jit(solution)/shard_map/ppermute | solution.py:332
  36.8 2.2 collective-permute-start.2
  39.7 3.1 fusion.30
  44.7 3.5 %all-to-all-start.1 = ((bf16[4,256,384]{2,1,0:T(8,128)(2,1)}), bf16[4,256,384]{2,1,0:T(8,128)(2,1)S(1)}, u32[]{:S(2)}, u32[]{:S(2)}) async-start(bf16[4,256,384]{2,1,0:T(8,128)(2,1)} %broadcast_in_dim.21), calls=%async_computation.1 | async-start | bytes 1572864 | tf_op jit(solution)/shard_map/all_to_all | solution.py:262
  54.5 4.2 %collective-permute-done = bf16[128,1024]{1,0:T(8,128)(2,1)S(1)} collective-permute-done((bf16[128,1024]{1,0:T(8,128)(2,1)}, bf16[128,1024]{1,0:T(8,128)(2,1)S(1)}, u32[]{:S(2)}, u32[]{:S(2)}) %collective-permute-start) | collective-permute-done | bytes 262176 | tf_op jit(solution)/shard_map/ppermute | solution.py:25
  58.7 2.3 collective-permute-start.43
  64.5 3.3 all-to-all-done.1
  67.8 4.2 %all-to-all-start.2 = ((bf16[8,32,1152]{2,1,0:T(8,128)(2,1)}), bf16[8,32,1152]{2,1,0:T(8,128)(2,1)}, u32[]{:S(2)}, u32[]{:S(2)}) async-start(bf16[8,32,1152]{2,1,0:T(8,128)(2,1)} %copy.64), calls=%async_computation.2 | async-start | bytes 1179648 | tf_op jit(solution)/shard_map/all_to_all | solution.py:267
  72.0 8.2 %project.1 = (bf16[1024,1024]{1,0:T(8,128)(2,1)}, bf16[1024,128]{1,0:T(8,128)(2,1)}, bf16[1024,128]{1,0:T(8,128)(2,1)}, bf16[1024,128]{1,0:T(8,128)(2,1)}) custom-call(bf16[1024,1024]{1,0:T(8,128)(2,1)} %copy-done.2, bf16[1024,384]{1,0:T(8,128)(2,1)} %bitcast.60, f32[1024,128]{1,0:T(8,128)} %get-tuple-element.134.cos_ref, f32[1024,128]{1,0:T(8,128)} %get-tuple-element.133.sin_ref), custom_call_target="tpu_custom_call" | custom-call | tf_op jit(solution)/shard_map/project/pallas_call | solution.py:79
  84.4 2.8 broadcast_in_dim.49
  87.1 6.5 %all-to-all-start.3 = ((bf16[4,256,1152]{2,1,0:T(8,128)(2,1)}), bf16[4,256,1152]{2,1,0:T(8,128)(2,1)}, u32[]{:S(2)}, u32[]{:S(2)}) async-start(bf16[4,256,1152]{2,1,0:T(8,128)(2,1)} %broadcast_in_dim.49), calls=%async_computation.3 | async-start | bytes 4718592 | tf_op jit(solution)/shard_map/all_to_all | solution.py:262
  94.2 4.2 %attend.1 = (bf16[1024,128]{1,0:T(8,128)(2,1)}, f32[1024,128]{1,0:T(8,128)}) custom-call(s32[2]{0:T(128)} %pad_add_fusion.at_ref, bf16[1024,128]{1,0:T(8,128)(2,1)} %get-tuple-element.17.q_ref, bf16[1024,128]{1,0:T(8,128)(2,1)} %get-tuple-element.18.k_ref, bf16[1024,128]{1,0:T(8,128)(2,1)} %get-tuple-element.19.v_ref, bf16[64,256]{1,0:T(8,128)(2,1)} %copy-done.15, ...), custom_call_target="tpu_custom_call" | custom-call | tf_op jit(solution)/shard_map/attend/pallas_call | solution.py:157
  106.6 3.8 %collective-permute-done.42 = bf16[128,1024]{1,0:T(8,128)(2,1)S(1)} collective-permute-done((bf16[128,1024]{1,0:T(8,128)(2,1)S(1)}, bf16[128,1024]{1,0:T(8,128)(2,1)S(1)}, u32[]{:S(2)}, u32[]{:S(2)}) %collective-permute-start.42) | collective-permute-done | bytes 262176 | tf_op jit(solution)/shard_map/ppermute | solution.py:25
  114.0 5.0 %collective-permute-done.22 = bf16[128,1024]{0,1:T(8,128)(2,1)S(1)} collective-permute-done((bf16[128,1024]{0,1:T(8,128)(2,1)S(1)}, bf16[128,1024]{0,1:T(8,128)(2,1)S(1)}, u32[]{:S(2)}, u32[]{:S(2)}) %collective-permute-start.22) | collective-permute-done | bytes 262176 | tf_op jit(solution)/shard_map/ppermute | solution.py:25
  118.9 2.3 collective-permute-done.24
  121.8 2.7 collective-permute-start.29
  125.6 6.4 %collective-permute-done.29 = bf16[128,1024]{0,1:T(8,128)(2,1)S(1)} collective-permute-done((bf16[128,1024]{0,1:T(8,128)(2,1)S(1)}, bf16[128,1024]{0,1:T(8,128)(2,1)S(1)}, u32[]{:S(2)}, u32[]{:S(2)}) %collective-permute-start.29) | collective-permute-done | bytes 262176 | tf_op jit(solution)/shard_map/ppermute | solution.py:29
  132.0 4.7 %collective-permute-done.28 = bf16[128,1024]{0,1:T(8,128)(2,1)S(1)} collective-permute-done((bf16[128,1024]{0,1:T(8,128)(2,1)S(1)}, bf16[128,1024]{0,1:T(8,128)(2,1)S(1)}, u32[]{:S(2)}, u32[]{:S(2)}) %collective-permute-start.28) | collective-permute-done | bytes 262176 | tf_op jit(solution)/shard_map/ppermute | solution.py:25
  138.9 8.5 %all-to-all-done.3 = bf16[4,256,1152]{2,1,0:T(8,128)(2,1)} async-done(((bf16[4,256,1152]{2,1,0:T(8,128)(2,1)}), bf16[4,256,1152]{2,1,0:T(8,128)(2,1)}, u32[]{:S(2)}, u32[]{:S(2)}) %all-to-all-start.3) | async-done | bytes 2359328 | tf_op jit(solution)/shard_map/all_to_all | solution.py:262
  147.5 3.4 fusion.7
  150.9 3.9 %fusion.5 = (bf16[1024,384]{0,1:T(8,128)(2,1)S(1)}, bf16[1024,384]{0,1:T(8,128)(2,1)S(1)}, bf16[1024,384]{0,1:T(8,128)(2,1)}) fusion(f32[1024,768]{0,1:T(8,128)S(1)} %fusion.7, bf16[1024,1024]{1,0:T(8,128)(2,1)S(1)} %copy-done.23, bf16[1024,1152]{1,0:T(8,128)(2,1)} %bitcast.14), kind=kOutput, calls=%fused_computation.15 | convolution fusion | flops 811597824 | bytes 8388608 | tf_op jit(solution)/shard_map/dot_general | solution.py:286
  154.9 3.8 %convolution_convert_fusion.3 = bf16[1024,1024]{0,1:T(8,128)(2,1)S(1)} fusion(bf16[1024,1152]{1,0:T(8,128)(2,1)} %bitcast.14, bf16[1024,384]{0,1:T(8,128)(2,1)S(1)} %get-tuple-element.79, bf16[1024,384]{0,1:T(8,128)(2,1)S(1)} %get-tuple-element.78), kind=kOutput, calls=%fused_computation.6 | convolution fusion | flops 1614807040 | bytes 5242880 | tf_op jit(solution)/shard_map/dot_general | solution.py:123
  167.2 9.8 %collective-permute-done.50 = bf16[128,1024]{0,1:T(8,128)(2,1)S(1)} collective-permute-done((bf16[128,1024]{0,1:T(8,128)(2,1)}, bf16[128,1024]{0,1:T(8,128)(2,1)S(1)}, u32[]{:S(2)}, u32[]{:S(2)}) %collective-permute-start.50) | collective-permute-done | bytes 262176 | tf_op jit(solution)/shard_map/ppermute | solution.py:25
  180.0 2.6 collective-permute-start.57
  183.6 6.6 %collective-permute-done.57 = bf16[128,1024]{0,1:T(8,128)(2,1)S(1)} collective-permute-done((bf16[128,1024]{0,1:T(8,128)(2,1)S(1)}, bf16[128,1024]{0,1:T(8,128)(2,1)S(1)}, u32[]{:S(2)}, u32[]{:S(2)}) %collective-permute-start.57) | collective-permute-done | bytes 262176 | tf_op jit(solution)/shard_map/ppermute | solution.py:29
  190.2 3.9 %collective-permute-done.56 = bf16[128,1024]{0,1:T(8,128)(2,1)S(1)} collective-permute-done((bf16[128,1024]{0,1:T(8,128)(2,1)S(1)}, bf16[128,1024]{0,1:T(8,128)(2,1)S(1)}, u32[]{:S(2)}, u32[]{:S(2)}) %collective-permute-start.56) | collective-permute-done | bytes 262176 | tf_op jit(solution)/shard_map/ppermute | solution.py:25
  197.8 7.2 %attend_back.1 = (bf16[1024,128]{1,0:T(8,128)(2,1)}, f32[1152,128]{1,0:T(8,128)}, f32[1152,128]{1,0:T(8,128)}) custom-call(s32[2]{0:T(128)} %pad_add_fusion.at_ref, bf16[1024,128]{1,0:T(8,128)(2,1)} %get-tuple-element.17.q_ref, bf16[1024,128]{1,0:T(8,128)(2,1)} %get-tuple-element.18.k_ref, bf16[1024,128]{1,0:T(8,128)(2,1)} %get-tuple-element.19.v_ref, ...), custom_call_target="tpu_custom_call" | custom-call | tf_op jit(solution)/shard_map/attend_back/pallas_call | solution.py:213
  207.1 4.5 %collective-permute-start.62 = (bf16[64,256]{1,0:T(8,128)(2,1)S(1)}, bf16[64,256]{1,0:T(8,128)(2,1)S(1)}, u32[]{:S(2)}, u32[]{:S(2)}) collective-permute-start(bf16[64,256]{1,0:T(8,128)(2,1)S(1)} %get-tuple-element.113), channel_id=1, source_target_pairs={{0,8},{8,16},{16,24},{1,9},{9,17},{17,25},{2,10},{10,18},{18,26},{... | collective-permute-start | bytes 98312 | tf_op jit(solution)/shard_map/ppermute | solution.py:257
  213.8 2.9 finish.1
  216.8 3.9 %convolution_convert_fusion.6 = bf16[1024,384]{1,0:T(8,128)(2,1)} fusion(bf16[1024,1024]{1,0:T(8,128)(2,1)} %get-tuple-element.25, bf16[1024,384]{1,0:T(8,128)(2,1)} %finish.1), kind=kOutput, calls=%fused_computation.22 | convolution fusion | flops 805699584 | bytes 3670016 | tf_op jit(solution)/shard_map/dot_general | solution.py:127
  220.7 4.4 %all-to-all-start.4 = ((bf16[32,32,384]{2,1,0:T(8,128)(2,1)}), bf16[32,32,384]{2,1,0:T(8,128)(2,1)}, u32[]{:S(2)}, u32[]{:S(2)}) async-start(bf16[32,32,384]{2,1,0:T(8,128)(2,1)} %bitcast.69), calls=%async_computation.4 | async-start | bytes 1572864 | tf_op jit(solution)/shard_map/all_to_all | solution.py:291
  225.2 3.0 convolution_convert_fusion.5
  231.7 4.3 %copy.70 = bf16[1024,1152]{1,0:T(8,128)(2,1)} copy(bf16[1024,1152]{0,1:T(8,128)(2,1)} %pad_maximum_fusion) | data formatting | bytes 4718592 | tf_op jit(solution)/shard_map/concatenate | solution.py:375
  236.0 9.7 %all-to-all-done.4 = bf16[32,32,384]{2,1,0:T(8,128)(2,1)} async-done(((bf16[32,32,384]{2,1,0:T(8,128)(2,1)}), bf16[32,32,384]{2,1,0:T(8,128)(2,1)}, u32[]{:S(2)}, u32[]{:S(2)}) %all-to-all-start.4) | async-done | bytes 786464 | tf_op jit(solution)/shard_map/all_to_all | solution.py:291
  245.7 3.7 %all-to-all-start.5 = ((bf16[32,32,1152]{2,1,0:T(8,128)(2,1)}), bf16[32,32,1152]{2,1,0:T(8,128)(2,1)}, u32[]{:S(2)}, u32[]{:S(2)}) async-start(bf16[32,32,1152]{2,1,0:T(8,128)(2,1)} %bitcast.59), calls=%async_computation.5 | async-start | bytes 4718592 | tf_op jit(solution)/shard_map/all_to_all | solution.py:291
  249.5 2.7 convolution_convert_fusion
  257.2 6.9 %collective-permute-start.74 = (bf16[32,1024]{1,0:T(8,128)(2,1)S(1)}, bf16[32,1024]{1,0:T(8,128)(2,1)S(1)}, u32[]{:S(2)}, u32[]{:S(2)}) collective-permute-start(bf16[32,1024]{1,0:T(8,128)(2,1)S(1)} %get-tuple-element.123), channel_id=1, source_target_pairs={{0,3},{1,7},{2,11},{3,15},{4,19},{5,23},{6,27},{7,31},{8,0},{9,4},... | collective-permute-start | bytes 196616 | tf_op jit(solution)/shard_map/ppermute | solution.py:394
  264.6 6.0 %collective-permute-start.72 = (bf16[32,1024]{1,0:T(8,128)(2,1)S(1)}, bf16[32,1024]{1,0:T(8,128)(2,1)S(1)}, u32[]{:S(2)}, u32[]{:S(2)}) collective-permute-start(bf16[32,1024]{1,0:T(8,128)(2,1)S(1)} %get-tuple-element.125), channel_id=1, source_target_pairs={{0,1},{1,5},{2,9},{3,13},{4,17},{5,21},{6,25},{7,29},{8,2},{9,6},{... | collective-permute-start | bytes 196616 | tf_op jit(solution)/shard_map/ppermute | solution.py:394
  270.7 7.7 %collective-permute-start.66 = (bf16[128,1024]{0,1:T(8,128)(2,1)S(1)}, bf16[128,1024]{0,1:T(8,128)(2,1)S(1)}, u32[]{:S(2)}, u32[]{:S(2)}) collective-permute-start(bf16[128,1024]{0,1:T(8,128)(2,1)S(1)} %get-tuple-element.85), channel_id=1, source_target_pairs={{0,1},{1,0},{2,3},{3,2},{4,5},{5,4},{6,7},{7,6},{8,9},{9,8},{10,11... | collective-permute-start | bytes 786440 | tf_op jit(solution)/shard_map/ppermute | solution.py:25
  280.4 34.9 %collective-permute-start.70 = (bf16[128,1024]{0,1:T(8,128)(2,1)S(1)}, bf16[128,1024]{0,1:T(8,128)(2,1)S(1)}, u32[]{:S(2)}, u32[]{:S(2)}) collective-permute-start(bf16[128,1024]{0,1:T(8,128)(2,1)S(1)} %get-tuple-element.86), channel_id=1, source_target_pairs={{0,5},{1,4},{4,1},{5,0},{2,7},{3,6},{6,3},{7,2},{8,13},{9,12},{12,... | collective-permute-start | bytes 786440 | tf_op jit(solution)/shard_map/ppermute | solution.py:29
  319.8 2.7 collective-permute-done.70
  323.3 3.5 %collective-permute-done.68 = bf16[128,1024]{0,1:T(8,128)(2,1)S(1)} collective-permute-done((bf16[128,1024]{0,1:T(8,128)(2,1)S(1)}, bf16[128,1024]{0,1:T(8,128)(2,1)S(1)}, u32[]{:S(2)}, u32[]{:S(2)}) %collective-permute-start.68) | collective-permute-done | bytes 262176 | tf_op jit(solution)/shard_map/ppermute | solution.py:25
  327.1 5.9 %collective-permute-done.36 = bf16[128,1024]{0,1:T(8,128)(2,1)S(1)} collective-permute-done((bf16[128,1024]{0,1:T(8,128)(2,1)S(1)}, bf16[128,1024]{0,1:T(8,128)(2,1)S(1)}, u32[]{:S(2)}, u32[]{:S(2)}) %collective-permute-start.36) | collective-permute-done | bytes 262176 | tf_op jit(solution)/shard_map/ppermute | solution.py:25
  333.2 4.4 %collective-permute-done.38 = bf16[128,1024]{0,1:T(8,128)(2,1)S(1)} collective-permute-done((bf16[128,1024]{0,1:T(8,128)(2,1)S(1)}, bf16[128,1024]{0,1:T(8,128)(2,1)S(1)}, u32[]{:S(2)}, u32[]{:S(2)}) %collective-permute-start.38) | collective-permute-done | bytes 262176 | tf_op jit(solution)/shard_map/ppermute | solution.py:25
  (306 shorter events, 94.9 us)
Async XLA Ops:
  0.7 26.8 %collective-permute-start.10 = (s32[1,2,128]{2,0,1:T(1,128)}, s32[1,2,128]{2,0,1:T(1,128)S(1)}, u32[]{:S(2)}, u32[]{:S(2)}) collective-permute-start(s32[1,2,128]{2,0,1:T(1,128)} %bitcast.72), channel_id=1, source_target_pairs={{0,2},{2,0},{1,3},{3,1},{4,6},{6,4},{5,7},{7,5},{8,10},{10,8},{9,1... | collective-permute-start | bytes 3080 | tf_op jit(solution)/shard_map/ppermute | solution.py:25
  1.2 24.5 %collective-permute-start.9 = (s32[1,2,128]{2,0,1:T(1,128)}, s32[1,2,128]{2,0,1:T(1,128)S(1)}, u32[]{:S(2)}, u32[]{:S(2)}) collective-permute-start(s32[1,2,128]{2,0,1:T(1,128)} %bitcast.73), channel_id=1, source_target_pairs={{0,5},{1,4},{4,1},{5,0},{2,7},{3,6},{6,3},{7,2},{8,13},{9,12},{12,... | collective-permute-start | bytes 3080 | tf_op jit(solution)/shard_map/ppermute | solution.py:29
  4.7 21.3 %collective-permute-start.8 = (s32[1,2,128]{2,0,1:T(1,128)}, s32[1,2,128]{2,0,1:T(1,128)S(1)}, u32[]{:S(2)}, u32[]{:S(2)}) collective-permute-start(s32[1,2,128]{2,0,1:T(1,128)} %bitcast.74), channel_id=1, source_target_pairs={{0,4},{4,0},{1,5},{5,1},{2,6},{6,2},{3,7},{7,3},{8,12},{12,8},{9,1... | collective-permute-start | bytes 3080 | tf_op jit(solution)/shard_map/ppermute | solution.py:25
  5.3 21.0 %collective-permute-start.7 = (s32[1,2,128]{2,0,1:T(1,128)}, s32[1,2,128]{2,0,1:T(1,128)}, u32[]{:S(2)}, u32[]{:S(2)}) collective-permute-start(s32[1,2,128]{2,0,1:T(1,128)} %bitcast.75), channel_id=1, source_target_pairs={{0,1},{1,0},{2,3},{3,2},{4,5},{5,4},{6,7},{7,6},{8,9},{9,8},{10,11... | collective-permute-start | bytes 3080 | tf_op jit(solution)/shard_map/ppermute | solution.py:25
  5.4 48.1 %collective-permute-start.17 = (bf16[32,1024]{1,0:T(8,128)(2,1)}, bf16[32,1024]{1,0:T(8,128)(2,1)S(1)}, u32[]{:S(2)}, u32[]{:S(2)}) collective-permute-start(bf16[32,1024]{1,0:T(8,128)(2,1)} %param.14), channel_id=1, source_target_pairs={{0,24},{1,0},{2,8},{3,16},{4,25},{5,1},{6,9},{7,17},{8,26},{9,2},{... | collective-permute-start | bytes 196616 | tf_op jit(solution)/shard_map/ppermute | solution.py:332
  14.0 28.8 %all-to-all-start = ((bf16[8,32,384]{2,1,0:T(8,128)(2,1)}), bf16[8,32,384]{2,1,0:T(8,128)(2,1)}, u32[]{:S(2)}, u32[]{:S(2)}) async-start(bf16[8,32,384]{2,1,0:T(8,128)(2,1)} %reshape.158), calls=%async_computation | async-start | bytes 393216 | tf_op jit(solution)/shard_map/all_to_all | solution.py:267
  26.3 10.6 %collective-permute-start.11 = (s32[1,2,128]{2,0,1:T(1,128)}, s32[1,2,128]{2,0,1:T(1,128)S(1)}, u32[]{:S(2)}, u32[]{:S(2)}) collective-permute-start(s32[1,2,128]{2,0,1:T(1,128)} %collective-permute-done.7), channel_id=1, source_target_pairs={{0,2},{2,0},{1,3},{3,1},{4,6},{6,4},{5,7},{7,5},{8,10},{10,8},{9,1... | collective-permute-start | bytes 3080 | tf_op jit(solution)/shard_map/ppermute | solution.py:25
  27.5 22.8 %collective-permute-start.16 = (bf16[32,1024]{1,0:T(8,128)(2,1)}, bf16[32,1024]{1,0:T(8,128)(2,1)S(1)}, u32[]{:S(2)}, u32[]{:S(2)}) collective-permute-start(bf16[32,1024]{1,0:T(8,128)(2,1)} %param.14), channel_id=1, source_target_pairs={{0,0},{1,8},{2,16},{3,24},{4,1},{5,9},{6,17},{7,25},{8,2},{9,10},{... | collective-permute-start | bytes 196616 | tf_op jit(solution)/shard_map/ppermute | solution.py:332
  29.0 55.3 %collective-permute-start.19 = (bf16[32,1024]{1,0:T(8,128)(2,1)}, bf16[32,1024]{1,0:T(8,128)(2,1)S(1)}, u32[]{:S(2)}, u32[]{:S(2)}) collective-permute-start(bf16[32,1024]{1,0:T(8,128)(2,1)} %param.14), channel_id=1, source_target_pairs={{0,8},{1,16},{2,24},{3,0},{4,9},{5,17},{6,25},{7,1},{8,10},{9,18},... | collective-permute-start | bytes 196616 | tf_op jit(solution)/shard_map/ppermute | solution.py:332
  33.1 20.4 %collective-permute-start.18 = (bf16[32,1024]{1,0:T(8,128)(2,1)}, bf16[32,1024]{1,0:T(8,128)(2,1)}, u32[]{:S(2)}, u32[]{:S(2)}) collective-permute-start(bf16[32,1024]{1,0:T(8,128)(2,1)} %param.14), channel_id=1, source_target_pairs={{0,16},{1,24},{2,0},{3,8},{4,17},{5,25},{6,1},{7,9},{8,18},{9,26},... | collective-permute-start | bytes 196616 | tf_op jit(solution)/shard_map/ppermute | solution.py:332
  36.8 24.3 %collective-permute-start.2 = (bf16[128,1024]{1,0:T(8,128)(2,1)}, bf16[128,1024]{1,0:T(8,128)(2,1)}, u32[]{:S(2)}, u32[]{:S(2)}) collective-permute-start(bf16[128,1024]{1,0:T(8,128)(2,1)} %param.10), channel_id=1, source_target_pairs={{0,5},{1,4},{4,1},{5,0},{2,7},{3,6},{6,3},{7,2},{8,13},{9,12},{12,... | collective-permute-start | bytes 786440 | tf_op jit(solution)/shard_map/ppermute | solution.py:29
  44.7 23.1 %all-to-all-start.1 = ((bf16[4,256,384]{2,1,0:T(8,128)(2,1)}), bf16[4,256,384]{2,1,0:T(8,128)(2,1)S(1)}, u32[]{:S(2)}, u32[]{:S(2)}) async-start(bf16[4,256,384]{2,1,0:T(8,128)(2,1)} %broadcast_in_dim.21), calls=%async_computation.1 | async-start | bytes 1572864 | tf_op jit(solution)/shard_map/all_to_all | solution.py:262
  58.7 47.8 %collective-permute-start.43 = (bf16[128,1024]{1,0:T(8,128)(2,1)}, bf16[128,1024]{1,0:T(8,128)(2,1)}, u32[]{:S(2)}, u32[]{:S(2)}) collective-permute-start(bf16[128,1024]{1,0:T(8,128)(2,1)} %param.18), channel_id=1, source_target_pairs={{0,5},{1,4},{4,1},{5,0},{2,7},{3,6},{6,3},{7,2},{8,13},{9,12},{12,... | collective-permute-start | bytes 786440 | tf_op jit(solution)/shard_map/ppermute | solution.py:29
  62.8 38.3 %collective-permute-start.41 = (bf16[128,1024]{1,0:T(8,128)(2,1)}, bf16[128,1024]{1,0:T(8,128)(2,1)}, u32[]{:S(2)}, u32[]{:S(2)}) collective-permute-start(bf16[128,1024]{1,0:T(8,128)(2,1)} %param.18), channel_id=1, source_target_pairs={{0,1},{1,0},{2,3},{3,2},{4,5},{5,4},{6,7},{7,6},{8,9},{9,8},{10,11... | collective-permute-start | bytes 786440 | tf_op jit(solution)/shard_map/ppermute | solution.py:25
  67.8 16.6 %all-to-all-start.2 = ((bf16[8,32,1152]{2,1,0:T(8,128)(2,1)}), bf16[8,32,1152]{2,1,0:T(8,128)(2,1)}, u32[]{:S(2)}, u32[]{:S(2)}) async-start(bf16[8,32,1152]{2,1,0:T(8,128)(2,1)} %copy.64), calls=%async_computation.2 | async-start | bytes 1179648 | tf_op jit(solution)/shard_map/all_to_all | solution.py:267
  81.7 11.9 %collective-permute-start.14 = (bf16[64,256]{1,0:T(8,128)(2,1)S(1)}, bf16[64,256]{1,0:T(8,128)(2,1)S(1)}, u32[]{:S(2)}, u32[]{:S(2)}) collective-permute-start(bf16[64,256]{1,0:T(8,128)(2,1)S(1)} %pad_maximum_fusion.6), channel_id=1, source_target_pairs={{0,8},{8,16},{16,24},{1,9},{9,17},{17,25},{2,10},{10,18},{18,26},{... | collective-permute-start | bytes 98312 | tf_op jit(solution)/shard_map/ppermute | solution.py:257
  83.0 10.6 %collective-permute-start.15 = (bf16[64,256]{1,0:T(8,128)(2,1)S(1)}, bf16[64,256]{1,0:T(8,128)(2,1)S(1)}, u32[]{:S(2)}, u32[]{:S(2)}) collective-permute-start(bf16[64,256]{1,0:T(8,128)(2,1)S(1)} %pad_maximum_fusion.7), channel_id=1, source_target_pairs={{8,0},{16,8},{24,16},{9,1},{17,9},{25,17},{10,2},{18,10},{26,18},{... | collective-permute-start | bytes 98312 | tf_op jit(solution)/shard_map/ppermute | solution.py:257
  87.1 60.3 %all-to-all-start.3 = ((bf16[4,256,1152]{2,1,0:T(8,128)(2,1)}), bf16[4,256,1152]{2,1,0:T(8,128)(2,1)}, u32[]{:S(2)}, u32[]{:S(2)}) async-start(bf16[4,256,1152]{2,1,0:T(8,128)(2,1)} %broadcast_in_dim.49), calls=%async_computation.3 | async-start | bytes 4718592 | tf_op jit(solution)/shard_map/all_to_all | solution.py:262
  104.9 14.0 %collective-permute-start.22 = (bf16[128,1024]{0,1:T(8,128)(2,1)S(1)}, bf16[128,1024]{0,1:T(8,128)(2,1)S(1)}, u32[]{:S(2)}, u32[]{:S(2)}) collective-permute-start(bf16[128,1024]{0,1:T(8,128)(2,1)S(1)} %get-tuple-element.106), channel_id=1, source_target_pairs={{0,1},{1,0},{2,3},{3,2},{4,5},{5,4},{6,7},{7,6},{8,9},{9,8},{10,11... | collective-permute-start | bytes 786440 | tf_op jit(solution)/shard_map/ppermute | solution.py:25
  106.4 12.5 %collective-permute-start.26 = (bf16[128,1024]{0,1:T(8,128)(2,1)S(1)}, bf16[128,1024]{0,1:T(8,128)(2,1)S(1)}, u32[]{:S(2)}, u32[]{:S(2)}) collective-permute-start(bf16[128,1024]{0,1:T(8,128)(2,1)S(1)} %get-tuple-element.107), channel_id=1, source_target_pairs={{0,5},{1,4},{4,1},{5,0},{2,7},{3,6},{6,3},{7,2},{8,13},{9,12},{12,... | collective-permute-start | bytes 786440 | tf_op jit(solution)/shard_map/ppermute | solution.py:29
  110.4 10.9 %collective-permute-start.24 = (bf16[128,1024]{0,1:T(8,128)(2,1)S(1)}, bf16[128,1024]{0,1:T(8,128)(2,1)S(1)}, u32[]{:S(2)}, u32[]{:S(2)}) collective-permute-start(bf16[128,1024]{0,1:T(8,128)(2,1)S(1)} %get-tuple-element.108), channel_id=1, source_target_pairs={{0,4},{4,0},{1,5},{5,1},{2,6},{6,2},{3,7},{7,3},{8,12},{12,8},{9,1... | collective-permute-start | bytes 786440 | tf_op jit(solution)/shard_map/ppermute | solution.py:25
  113.3 12.2 %collective-permute-start.47 = (bf16[128,1024]{1,0:T(8,128)(2,1)}, bf16[128,1024]{1,0:T(8,128)(2,1)S(1)}, u32[]{:S(2)}, u32[]{:S(2)}) collective-permute-start(bf16[128,1024]{1,0:T(8,128)(2,1)} %collective-permute-done.43), channel_id=1, source_target_pairs={{0,2},{2,0},{1,3},{3,1},{4,6},{6,4},{5,7},{7,5},{8,10},{10,8},{9,1... | collective-permute-start | bytes 786440 | tf_op jit(solution)/shard_map/ppermute | solution.py:25
  113.4 12.0 %collective-permute-start.46 = (bf16[128,1024]{1,0:T(8,128)(2,1)S(1)}, bf16[128,1024]{1,0:T(8,128)(2,1)S(1)}, u32[]{:S(2)}, u32[]{:S(2)}) collective-permute-start(bf16[128,1024]{1,0:T(8,128)(2,1)S(1)} %collective-permute-done.42), channel_id=1, source_target_pairs={{0,2},{2,0},{1,3},{3,1},{4,6},{6,4},{5,7},{7,5},{8,10},{10,8},{9,1... | collective-permute-start | bytes 786440 | tf_op jit(solution)/shard_map/ppermute | solution.py:25
  121.8 10.2 %collective-permute-start.29 = (bf16[128,1024]{0,1:T(8,128)(2,1)S(1)}, bf16[128,1024]{0,1:T(8,128)(2,1)S(1)}, u32[]{:S(2)}, u32[]{:S(2)}) collective-permute-start(bf16[128,1024]{0,1:T(8,128)(2,1)S(1)} %get-tuple-element.75), channel_id=1, source_target_pairs={{0,5},{1,4},{4,1},{5,0},{2,7},{3,6},{6,3},{7,2},{8,13},{9,12},{12,... | collective-permute-start | bytes 786440 | tf_op jit(solution)/shard_map/ppermute | solution.py:29
  124.6 12.1 %collective-permute-start.28 = (bf16[128,1024]{0,1:T(8,128)(2,1)S(1)}, bf16[128,1024]{0,1:T(8,128)(2,1)S(1)}, u32[]{:S(2)}, u32[]{:S(2)}) collective-permute-start(bf16[128,1024]{0,1:T(8,128)(2,1)S(1)} %get-tuple-element.75), channel_id=1, source_target_pairs={{0,4},{4,0},{1,5},{5,1},{2,6},{6,2},{3,7},{7,3},{8,12},{12,8},{9,1... | collective-permute-start | bytes 786440 | tf_op jit(solution)/shard_map/ppermute | solution.py:25
  125.2 11.5 %collective-permute-start.27 = (bf16[128,1024]{0,1:T(8,128)(2,1)S(1)}, bf16[128,1024]{0,1:T(8,128)(2,1)S(1)}, u32[]{:S(2)}, u32[]{:S(2)}) collective-permute-start(bf16[128,1024]{0,1:T(8,128)(2,1)S(1)} %get-tuple-element.75), channel_id=1, source_target_pairs={{0,1},{1,0},{2,3},{3,2},{4,5},{5,4},{6,7},{7,6},{8,9},{9,8},{10,11... | collective-permute-start | bytes 786440 | tf_op jit(solution)/shard_map/ppermute | solution.py:25
  125.5 12.0 %collective-permute-start.30 = (bf16[128,1024]{0,1:T(8,128)(2,1)S(1)}, bf16[128,1024]{0,1:T(8,128)(2,1)S(1)}, u32[]{:S(2)}, u32[]{:S(2)}) collective-permute-start(bf16[128,1024]{0,1:T(8,128)(2,1)S(1)} %get-tuple-element.75), channel_id=1, source_target_pairs={{0,2},{2,0},{1,3},{3,1},{4,6},{6,4},{5,7},{7,5},{8,10},{10,8},{9,1... | collective-permute-start | bytes 786440 | tf_op jit(solution)/shard_map/ppermute | solution.py:25
  162.9 14.2 %collective-permute-start.50 = (bf16[128,1024]{0,1:T(8,128)(2,1)}, bf16[128,1024]{0,1:T(8,128)(2,1)S(1)}, u32[]{:S(2)}, u32[]{:S(2)}) collective-permute-start(bf16[128,1024]{0,1:T(8,128)(2,1)} %get-tuple-element.92), channel_id=1, source_target_pairs={{0,1},{1,0},{2,3},{3,2},{4,5},{5,4},{6,7},{7,6},{8,9},{9,8},{10,11... | collective-permute-start | bytes 786440 | tf_op jit(solution)/shard_map/ppermute | solution.py:25
  164.5 12.5 %collective-permute-start.54 = (bf16[128,1024]{0,1:T(8,128)(2,1)}, bf16[128,1024]{0,1:T(8,128)(2,1)}, u32[]{:S(2)}, u32[]{:S(2)}) collective-permute-start(bf16[128,1024]{0,1:T(8,128)(2,1)} %get-tuple-element.93), channel_id=1, source_target_pairs={{0,5},{1,4},{4,1},{5,0},{2,7},{3,6},{6,3},{7,2},{8,13},{9,12},{12,... | collective-permute-start | bytes 786440 | tf_op jit(solution)/shard_map/ppermute | solution.py:29
  166.0 12.4 %collective-permute-start.52 = (bf16[128,1024]{0,1:T(8,128)(2,1)}, bf16[128,1024]{0,1:T(8,128)(2,1)}, u32[]{:S(2)}, u32[]{:S(2)}) collective-permute-start(bf16[128,1024]{0,1:T(8,128)(2,1)} %get-tuple-element.94), channel_id=1, source_target_pairs={{0,4},{4,0},{1,5},{5,1},{2,6},{6,2},{3,7},{7,3},{8,12},{12,8},{9,1... | collective-permute-start | bytes 786440 | tf_op jit(solution)/shard_map/ppermute | solution.py:25
  182.7 11.4 %collective-permute-start.56 = (bf16[128,1024]{0,1:T(8,128)(2,1)S(1)}, bf16[128,1024]{0,1:T(8,128)(2,1)S(1)}, u32[]{:S(2)}, u32[]{:S(2)}) collective-permute-start(bf16[128,1024]{0,1:T(8,128)(2,1)S(1)} %get-tuple-element.72), channel_id=1, source_target_pairs={{0,4},{4,0},{1,5},{5,1},{2,6},{6,2},{3,7},{7,3},{8,12},{12,8},{9,1... | collective-permute-start | bytes 786440 | tf_op jit(solution)/shard_map/ppermute | solution.py:25
  183.2 10.9 %collective-permute-start.55 = (bf16[128,1024]{0,1:T(8,128)(2,1)S(1)}, bf16[128,1024]{0,1:T(8,128)(2,1)S(1)}, u32[]{:S(2)}, u32[]{:S(2)}) collective-permute-start(bf16[128,1024]{0,1:T(8,128)(2,1)S(1)} %get-tuple-element.72), channel_id=1, source_target_pairs={{0,1},{1,0},{2,3},{3,2},{4,5},{5,4},{6,7},{7,6},{8,9},{9,8},{10,11... | collective-permute-start | bytes 786440 | tf_op jit(solution)/shard_map/ppermute | solution.py:25
  183.6 11.3 %collective-permute-start.58 = (bf16[128,1024]{0,1:T(8,128)(2,1)S(1)}, bf16[128,1024]{0,1:T(8,128)(2,1)S(1)}, u32[]{:S(2)}, u32[]{:S(2)}) collective-permute-start(bf16[128,1024]{0,1:T(8,128)(2,1)S(1)} %get-tuple-element.72), channel_id=1, source_target_pairs={{0,2},{2,0},{1,3},{3,1},{4,6},{6,4},{5,7},{7,5},{8,10},{10,8},{9,1... | collective-permute-start | bytes 786440 | tf_op jit(solution)/shard_map/ppermute | solution.py:25
  220.7 25.0 %all-to-all-start.4 = ((bf16[32,32,384]{2,1,0:T(8,128)(2,1)}), bf16[32,32,384]{2,1,0:T(8,128)(2,1)}, u32[]{:S(2)}, u32[]{:S(2)}) async-start(bf16[32,32,384]{2,1,0:T(8,128)(2,1)} %bitcast.69), calls=%async_computation.4 | async-start | bytes 1572864 | tf_op jit(solution)/shard_map/all_to_all | solution.py:291
  245.7 97.4 %all-to-all-start.5 = ((bf16[32,32,1152]{2,1,0:T(8,128)(2,1)}), bf16[32,32,1152]{2,1,0:T(8,128)(2,1)}, u32[]{:S(2)}, u32[]{:S(2)}) async-start(bf16[32,32,1152]{2,1,0:T(8,128)(2,1)} %bitcast.59), calls=%async_computation.5 | async-start | bytes 4718592 | tf_op jit(solution)/shard_map/all_to_all | solution.py:291
  252.7 11.9 %collective-permute-start.37 = (bf16[128,1024]{0,1:T(8,128)(2,1)S(1)}, bf16[128,1024]{0,1:T(8,128)(2,1)S(1)}, u32[]{:S(2)}, u32[]{:S(2)}) collective-permute-start(bf16[128,1024]{0,1:T(8,128)(2,1)S(1)} %get-tuple-element.97), channel_id=1, source_target_pairs={{0,2},{2,0},{1,3},{3,1},{4,6},{6,4},{5,7},{7,5},{8,10},{10,8},{9,1... | collective-permute-start | bytes 786440 | tf_op jit(solution)/shard_map/ppermute | solution.py:25
  256.2 14.4 %collective-permute-start.35 = (bf16[128,1024]{0,1:T(8,128)(2,1)S(1)}, bf16[128,1024]{0,1:T(8,128)(2,1)S(1)}, u32[]{:S(2)}, u32[]{:S(2)}) collective-permute-start(bf16[128,1024]{0,1:T(8,128)(2,1)S(1)} %get-tuple-element.98), channel_id=1, source_target_pairs={{0,2},{2,0},{1,3},{3,1},{4,6},{6,4},{5,7},{7,5},{8,10},{10,8},{9,1... | collective-permute-start | bytes 786440 | tf_op jit(solution)/shard_map/ppermute | solution.py:25
  256.6 14.1 %collective-permute-start.71 = (bf16[32,1024]{1,0:T(8,128)(2,1)S(1)}, bf16[32,1024]{1,0:T(8,128)(2,1)S(1)}, u32[]{:S(2)}, u32[]{:S(2)}) collective-permute-start(bf16[32,1024]{1,0:T(8,128)(2,1)S(1)} %get-tuple-element.122), channel_id=1, source_target_pairs={{0,0},{1,4},{2,8},{3,12},{4,16},{5,20},{6,24},{7,28},{8,1},{9,5},{... | collective-permute-start | bytes 196616 | tf_op jit(solution)/shard_map/ppermute | solution.py:394
  257.2 23.1 %collective-permute-start.74 = (bf16[32,1024]{1,0:T(8,128)(2,1)S(1)}, bf16[32,1024]{1,0:T(8,128)(2,1)S(1)}, u32[]{:S(2)}, u32[]{:S(2)}) collective-permute-start(bf16[32,1024]{1,0:T(8,128)(2,1)S(1)} %get-tuple-element.123), channel_id=1, source_target_pairs={{0,3},{1,7},{2,11},{3,15},{4,19},{5,23},{6,27},{7,31},{8,0},{9,4},... | collective-permute-start | bytes 196616 | tf_op jit(solution)/shard_map/ppermute | solution.py:394
  264.2 51.1 %collective-permute-start.73 = (bf16[32,1024]{1,0:T(8,128)(2,1)S(1)}, bf16[32,1024]{1,0:T(8,128)(2,1)S(1)}, u32[]{:S(2)}, u32[]{:S(2)}) collective-permute-start(bf16[32,1024]{1,0:T(8,128)(2,1)S(1)} %get-tuple-element.124), channel_id=1, source_target_pairs={{0,2},{1,6},{2,10},{3,14},{4,18},{5,22},{6,26},{7,30},{8,3},{9,7},... | collective-permute-start | bytes 196616 | tf_op jit(solution)/shard_map/ppermute | solution.py:394
  264.6 52.3 %collective-permute-start.72 = (bf16[32,1024]{1,0:T(8,128)(2,1)S(1)}, bf16[32,1024]{1,0:T(8,128)(2,1)S(1)}, u32[]{:S(2)}, u32[]{:S(2)}) collective-permute-start(bf16[32,1024]{1,0:T(8,128)(2,1)S(1)} %get-tuple-element.125), channel_id=1, source_target_pairs={{0,1},{1,5},{2,9},{3,13},{4,17},{5,21},{6,25},{7,29},{8,2},{9,6},{... | collective-permute-start | bytes 196616 | tf_op jit(solution)/shard_map/ppermute | solution.py:394
  270.6 47.1 %collective-permute-start.64 = (bf16[128,1024]{0,1:T(8,128)(2,1)S(1)}, bf16[128,1024]{0,1:T(8,128)(2,1)S(1)}, u32[]{:S(2)}, u32[]{:S(2)}) collective-permute-start(bf16[128,1024]{0,1:T(8,128)(2,1)S(1)} %get-tuple-element.81), channel_id=1, source_target_pairs={{0,2},{2,0},{1,3},{3,1},{4,6},{6,4},{5,7},{7,5},{8,10},{10,8},{9,1... | collective-permute-start | bytes 786440 | tf_op jit(solution)/shard_map/ppermute | solution.py:25
  270.7 47.0 %collective-permute-start.66 = (bf16[128,1024]{0,1:T(8,128)(2,1)S(1)}, bf16[128,1024]{0,1:T(8,128)(2,1)S(1)}, u32[]{:S(2)}, u32[]{:S(2)}) collective-permute-start(bf16[128,1024]{0,1:T(8,128)(2,1)S(1)} %get-tuple-element.85), channel_id=1, source_target_pairs={{0,1},{1,0},{2,3},{3,2},{4,5},{5,4},{6,7},{7,6},{8,9},{9,8},{10,11... | collective-permute-start | bytes 786440 | tf_op jit(solution)/shard_map/ppermute | solution.py:25
  280.4 42.1 %collective-permute-start.70 = (bf16[128,1024]{0,1:T(8,128)(2,1)S(1)}, bf16[128,1024]{0,1:T(8,128)(2,1)S(1)}, u32[]{:S(2)}, u32[]{:S(2)}) collective-permute-start(bf16[128,1024]{0,1:T(8,128)(2,1)S(1)} %get-tuple-element.86), channel_id=1, source_target_pairs={{0,5},{1,4},{4,1},{5,0},{2,7},{3,6},{6,3},{7,2},{8,13},{9,12},{12,... | collective-permute-start | bytes 786440 | tf_op jit(solution)/shard_map/ppermute | solution.py:29
  315.3 11.5 %collective-permute-start.68 = (bf16[128,1024]{0,1:T(8,128)(2,1)S(1)}, bf16[128,1024]{0,1:T(8,128)(2,1)S(1)}, u32[]{:S(2)}, u32[]{:S(2)}) collective-permute-start(bf16[128,1024]{0,1:T(8,128)(2,1)S(1)} %get-tuple-element.87), channel_id=1, source_target_pairs={{0,4},{4,0},{1,5},{5,1},{2,6},{6,2},{3,7},{7,3},{8,12},{12,8},{9,1... | collective-permute-start | bytes 786440 | tf_op jit(solution)/shard_map/ppermute | solution.py:25
  317.7 15.3 %collective-permute-start.36 = (bf16[128,1024]{0,1:T(8,128)(2,1)S(1)}, bf16[128,1024]{0,1:T(8,128)(2,1)S(1)}, u32[]{:S(2)}, u32[]{:S(2)}) collective-permute-start(bf16[128,1024]{0,1:T(8,128)(2,1)S(1)} %get-tuple-element.99), channel_id=1, source_target_pairs={{0,1},{1,0},{2,3},{3,2},{4,5},{5,4},{6,7},{7,6},{8,9},{9,8},{10,11... | collective-permute-start | bytes 786440 | tf_op jit(solution)/shard_map/ppermute | solution.py:25
  317.7 15.5 %collective-permute-start.40 = (bf16[128,1024]{0,1:T(8,128)(2,1)S(1)}, bf16[128,1024]{0,1:T(8,128)(2,1)S(1)}, u32[]{:S(2)}, u32[]{:S(2)}) collective-permute-start(bf16[128,1024]{0,1:T(8,128)(2,1)S(1)} %get-tuple-element.100), channel_id=1, source_target_pairs={{0,5},{1,4},{4,1},{5,0},{2,7},{3,6},{6,3},{7,2},{8,13},{9,12},{12,... | collective-permute-start | bytes 786440 | tf_op jit(solution)/shard_map/ppermute | solution.py:29
  322.5 15.1 %collective-permute-start.38 = (bf16[128,1024]{0,1:T(8,128)(2,1)S(1)}, bf16[128,1024]{0,1:T(8,128)(2,1)S(1)}, u32[]{:S(2)}, u32[]{:S(2)}) collective-permute-start(bf16[128,1024]{0,1:T(8,128)(2,1)S(1)} %get-tuple-element.101), channel_id=1, source_target_pairs={{0,4},{4,0},{1,5},{5,1},{2,6},{6,2},{3,7},{7,3},{8,12},{12,8},{9,1... | collective-permute-start | bytes 786440 | tf_op jit(solution)/shard_map/ppermute | solution.py:25
  (67 other events, 437.9 us)
